TPU v7x, 32 devices: a whole 2x2x4 slice. The times are simulated.
32 devices in a mesh: wide: 8 (over z, y), narrow: 4 (over x, core).
Axes of the slice: x: 2, y: 2, z: 4, core: 2. Of those that a mesh axis runs over, the one named last changes fastest.
Arguments:
- op_blocks: bfloat16 [512, 6, 192, 192], P('wide', None, 'narrow'), may hold values from -6 to 6
- prolong: bfloat16 [512, 9216], P('wide', 'narrow'), may hold values from -0.4375 to 0.4375
- col_index: int32 [512, 6], P('wide'), may hold values from 0 to 511, as said below
- slot_index: int32 [512, 6], P('wide'), may hold values from 0 to 7
- dest_owner: int32 [512, 1], P('wide'), may hold values from 0 to 7; in each aligned block of 64 rows (0 to 63, 64 to 127, ...) at most 16 rows name the same one
- dest_local: int32 [512], P('wide'), may hold values from 0 to 15
Outputs:
- coarse: float32 [128, 48, 384], P('wide', 'narrow')
Inputs may be any that keep to these rules, and one draw needn't show every extreme that they name: `col_index`: the first column of each row is the row itself; every column lies in the block rows of the same wide index or of the one just before or after it. `dest_owner`: among the 64 rows of one wide index no owner is named more than 16 times; some owner is named exactly 16 times.
All inputs are finite; a program needn't handle non-finite values.
Results may differ from a plain program's by a relative error of at most 0.0029.
Values may be sent and summed in bfloat16 or wider, within the bound.
A program may use at most 128 MiB of HBM per device.

v0:
```python
import jax
import jax.numpy as jnp
from jax import lax
from jax.sharding import PartitionSpec as P

B = 192
M = 48
KC = 8
AGG_DEV = 16


def padded(cells, sides, width):
    for axis, dim in sides:
        count = lax.axis_size(axis)
        ends = count - 1
        head = lax.slice_in_dim(cells, 0, width, axis=dim)
        tail = lax.slice_in_dim(cells, cells.shape[dim] - width, cells.shape[dim], axis=dim)
        cells = jnp.concatenate(
            [
                lax.ppermute(tail, axis, [(i, (i + 1) % count) for i in range(ends)]),
                cells,
                lax.ppermute(head, axis, [((i + 1) % count, i) for i in range(ends)]),
            ],
            axis=dim,
        )
    return cells


def pack_rows(values, owner, tags, wide_size, capacity):
    count_rows = owner.shape[0]
    targets = (owner[:, None] == jnp.arange(wide_size, dtype=jnp.int32)[None, :]).astype(jnp.int32)
    ranks = jnp.cumsum(targets, axis=0) - 1
    position = jnp.sum(ranks * targets, axis=1)
    slot_of = owner * capacity + position
    slot_ids = jnp.arange(wide_size * capacity, dtype=jnp.int32)
    match = (slot_of[None, :] == slot_ids[:, None]).astype(jnp.int32)
    source = jnp.sum(match * jnp.arange(count_rows, dtype=jnp.int32)[None, :], axis=1)
    filled = jnp.sum(match, axis=1) > 0
    picked = jnp.take(values, source, axis=0)
    value_mask = filled.reshape((-1,) + (1,) * (values.ndim - 1))
    packed = jnp.where(value_mask, picked, jnp.zeros_like(picked))
    labels = jnp.where(filled, jnp.take(tags, source, axis=0), -1)
    packed = packed.reshape((wide_size, capacity) + values.shape[1:])
    return (packed, labels.reshape((wide_size, capacity) + tags.shape[1:]))


def accumulate(received, labels, aggregates):
    flat = received.reshape((-1,) + received.shape[2:])
    selector = (
        labels.reshape(-1)[None, :] == jnp.arange(aggregates, dtype=jnp.int32)[:, None]
    ).astype(jnp.float32)
    return jnp.einsum("aj,jrc->arc", selector, flat, precision=lax.Precision.HIGHEST)


def slot_rows(projected, slot_index):
    count_rows = projected.shape[0]
    selector = (slot_index[:, :, None] == jnp.arange(KC, dtype=jnp.int32)[None, None, :]).astype(
        jnp.float32
    )
    return jnp.einsum(
        "iks,ikcm->icsm", selector, projected, precision=lax.Precision.HIGHEST
    ).reshape(count_rows, M, KC * M)


def on_device(op_blocks, prolong, col_index, slot_index, dest_owner, dest_local):
    count_rows = op_blocks.shape[0]
    count_terms = op_blocks.shape[1]
    part_rows = op_blocks.shape[2]
    wide_size = lax.axis_size("wide")
    wide_pos = lax.axis_index("wide")
    capacity = max(2, 2 * count_rows // wide_size)
    complete = lax.all_gather(prolong, "narrow", axis=1, tiled=True)
    nearby = padded(complete, (("wide", 0),), count_rows)
    local_cols = col_index - wide_pos * count_rows + count_rows
    picked = jnp.take(nearby, local_cols.reshape(-1), axis=0).reshape(count_rows, count_terms, B, M)
    applied = jnp.einsum(
        "ikrb,ikbm->ikrm", op_blocks, picked, preferred_element_type=jnp.float32
    ).astype(jnp.bfloat16)
    own_rows = prolong.reshape(count_rows, part_rows, M)
    projected = jnp.einsum("irc,ikrm->ikcm", own_rows, applied, preferred_element_type=jnp.float32)
    owner = dest_owner[:, 0]
    contrib = slot_rows(projected, slot_index)
    packed, labels = pack_rows(contrib, owner, dest_local, wide_size, capacity)
    received, got_labels = (
        lax.all_to_all(packed, "wide", split_axis=0, concat_axis=0, tiled=True),
        lax.all_to_all(labels, "wide", split_axis=0, concat_axis=0, tiled=True),
    )
    gathered_rows = accumulate(received, got_labels, AGG_DEV)
    coarse = lax.psum_scatter(gathered_rows, "narrow", scatter_dimension=1, tiled=True)
    return coarse


def solution(mesh):
    in_specs = (
        P("wide", None, "narrow", None),
        P("wide", "narrow"),
        P("wide", None),
        P("wide", None),
        P("wide", None),
        P("wide"),
    )
    out_specs = P("wide", "narrow", None)
    return jax.shard_map(
        on_device, mesh=mesh, in_specs=in_specs, out_specs=out_specs, check_vma=False
    )
```

profile of v0, /device:TPU:13, one launch (start us, length us, event | category | flops | bytes accessed | tf_op | source)
XLA Modules:
  0.0 439.6 jit_solution(7215567265443469886)
XLA Ops:
  6.5 0.7 all-gather.2.cloned.1.call-update
  7.3 0.7 fusion.21
  8.1 0.8 select_reduce_fusion.1
  8.9 0.7 multiply_add_fusion
  9.8 18.2 %all-gather.2.cloned.1.call-done = bf16[64,9216]{1,0:T(8,128)(2,1)} async-done(((bf16[64,2304]{1,0:T(8,128)(2,1)}), bf16[64,9216]{1,0:T(8,128)(2,1)}) %all-gather.2.cloned.1.call-update) | async-done | bytes 1179664 | tf_op jit(solution)/shard_map/all_gather | solution.py:72
  27.9 3.1 collective-permute-start
  31.0 2.2 collective-permute-start.1
  33.3 1.2 gather_fusion
  35.2 6.5 %all-to-all-start = ((s32[8,1,16]{2,1,0:T(1,128)}), s32[8,1,16]{2,1,0:T(1,128)S(1)}, u32[]{:S(2)}, u32[]{:S(2)}) async-start(s32[8,1,16]{2,1,0:T(1,128)} %bitcast.3), calls=%async_computation | async-start | bytes 8192 | tf_op jit(solution)/shard_map/all_to_all | solution.py:86
  41.8 2.9 reshape.190
  44.8 0.7 gt.35
  45.4 0.7 subtract_add_fusion
  46.4 0.7 compare_and_fusion
  47.1 0.7 copy.23
  47.8 1.4 copy.26
  49.8 32.9 %collective-permute-done = bf16[64,9216]{1,0:T(8,128)(2,1)S(1)} collective-permute-done((bf16[64,9216]{1,0:T(8,128)(2,1)}, bf16[64,9216]{1,0:T(8,128)(2,1)S(1)}, u32[]{:S(2)}, u32[]{:S(2)}) %collective-permute-start) | collective-permute-done | bytes 1179680 | tf_op jit(solution)/shard_map/ppermute | solution.py:20
  82.6 1.0 copy-done.2
  83.7 2.2 pad_maximum_fusion
  85.8 8.0 %gather_fusion.1 = bf16[384,9216]{1,0:T(8,128)(2,1)} fusion(bf16[192,9216]{1,0:T(8,128)(2,1)S(1)} %pad_maximum_fusion, s32[1024]{0:T(1024)S(1)} %pad_clamp_fusion), kind=kCustom, calls=%fused_computation.1 | custom fusion | bytes 14157312 | tf_op jit(solution)/shard_map/jit(_take)/gather | solution.py:75
  93.8 25.1 %gather.21 = bf16[64,6,192,48]{3,2,1,0:T(8,128)(2,1)} reshape(bf16[384,9216]{1,0:T(8,128)(2,1)} %gather_fusion.1) | data formatting | bytes 14155776 | tf_op jit(solution)/shard_map/jit(_take)/gather | solution.py:75
  119.0 16.8 %fusion.12 = f32[64,6,48,48]{2,3,1,0:T(8,128)} fusion(bf16[64,6,48,192]{3,2,1,0:T(8,128)(2,1)} %param.6, bf16[64,6,192,48]{3,2,1,0:T(8,128)(2,1)} %gather.21, pred[64,6]{1,0:T(8,128)(4,1)S(1)} %copy-done.5, bf16[64,48,48,1]{2,1,0,3:T(8,128)(2,1)S(1)} %copy-done.3), kind=kOutput, calls=%fused_computation.14 | convolution fusion | flops 429096960 | bytes 17990016 | tf_op jit(solution)/shard_map/irc,ikrm->ikcm/dot_general | solution.py:80
  135.8 11.4 %copy.27 = f32[64,6,48,48]{3,1,2,0:T(8,128)} copy(f32[64,6,48,48]{2,3,1,0:T(8,128)} %fusion.12) | data formatting | bytes 7077888 | tf_op jit(solution)/shard_map/irc,ikrm->ikcm/transpose | solution.py:80
  147.3 11.8 %convolution_bitcast_fusion = f32[64,48,8,48]{3,2,1,0:T(8,128)} fusion(f32[64,6,48,48]{3,1,2,0:T(8,128)} %copy.27, s32[64,6]{1,0:T(8,128)S(1)} %copy-done.4), kind=kOutput, calls=%fused_computation.12 | convolution fusion | flops 84937728 | bytes 8259072 | tf_op jit(solution)/shard_map/iks,ikcm->icsm/dot_general | solution.py:60
  159.0 10.7 %reshape.164 = f32[64,48,384]{2,1,0:T(8,128)} reshape(f32[64,48,8,48]{3,2,1,0:T(8,128)} %convolution_bitcast_fusion) | data formatting | bytes 9437184 | tf_op jit(solution)/shard_map/reshape | solution.py:62
  169.7 7.1 %gather_fusion.2 = f32[128,48,384]{2,1,0:T(8,128)} fusion(f32[64,48,384]{2,1,0:T(8,128)} %reshape.164, s32[1024]{0:T(1024)S(1)} %pad_clamp_fusion.1), kind=kCustom, calls=%fused_computation.2 | custom fusion | bytes 18874880 | tf_op jit(solution)/shard_map/jit(_take)/gather | solution.py:39
  176.8 11.6 %fusion.3 = f32[8,16,48,384]{3,1,2,0:T(8,128)} fusion(f32[8,16,48,384]{3,2,1,0:T(8,128)} %bitcast.34, pred[8,16]{1,0:T(8,128)(4,1)S(1)} %copy-done.6, pred[8,16]{1,0:T(8,128)(4,1)S(1)} %copy-done.7), kind=kLoop, calls=%fused_computation.7 | loop fusion | flops 4718592 | bytes 18874624 | tf_op jit(solution)/shard_map/jit(_where)/select_n | solution.py:41
  188.4 5.2 %all-to-all-start.1 = ((f32[8,16,48,384]{3,1,2,0:T(8,128)}), f32[8,16,48,384]{3,1,2,0:T(8,128)}, u32[]{:S(2)}, u32[]{:S(2)}) async-start(f32[8,16,48,384]{3,1,2,0:T(8,128)} %fusion.3), calls=%async_computation.1 | async-start | bytes 18874368 | tf_op jit(solution)/shard_map/all_to_all | solution.py:85
  194.1 0.7 reduce.5
  194.8 201.7 %all-to-all-done.1 = f32[8,16,48,384]{3,1,2,0:T(8,128)} async-done(((f32[8,16,48,384]{3,1,2,0:T(8,128)}), f32[8,16,48,384]{3,1,2,0:T(8,128)}, u32[]{:S(2)}, u32[]{:S(2)}) %all-to-all-start.1) | async-done | bytes 9437216 | tf_op jit(solution)/shard_map/all_to_all | solution.py:85
  396.6 5.0 %copy.29 = f32[8,16,48,384]{3,1,0,2:T(8,128)S(1)} copy(f32[8,16,48,384]{3,1,2,0:T(8,128)} %all-to-all-done.1) | data formatting | bytes 18874368 | tf_op jit(solution)/shard_map/all_to_all | solution.py:85
  401.6 4.2 fusion.23
  405.8 26.9 %reduce-scatter.2.cloned.1.call-done = f32[16,12,384]{2,0,1:T(8,128)} async-done(((f32[16,48,384]{2,0,1:T(8,128)}), f32[16,12,384]{2,0,1:T(8,128)}) %reduce-scatter.2.cloned.1.call-update) | async-done | bytes 294928 | tf_op jit(solution)/shard_map/reduce_scatter | solution.py:89
  (37 shorter events, 2.6 us)
Async XLA Ops:
  6.5 26.7 %copy-start = (s32[64]{0:T(128)S(1)}, s32[64]{0:T(128)}, u32[]{:S(2)}) copy-start(s32[64]{0:T(128)} %param.11) | copy-start | bytes 772
  6.5 21.4 %all-gather.2.cloned.1.call-start = ((), (), s32[]{:S(2)}) async-start(), calls=%async_computation.3 | async-start | bytes 1474560 | tf_op jit(solution)/shard_map/all_gather | solution.py:72
  27.9 54.7 %collective-permute-start = (bf16[64,9216]{1,0:T(8,128)(2,1)}, bf16[64,9216]{1,0:T(8,128)(2,1)S(1)}, u32[]{:S(2)}, u32[]{:S(2)}) collective-permute-start(bf16[64,9216]{1,0:T(8,128)(2,1)} %all-gather.2.cloned.1.call-done), channel_id=1, source_target_pairs={{0,4},{4,8},{8,12},{12,16},{16,20},{20,24},{24,28},{1,5},{5,9},{9,... | collective-permute-start | bytes 3538952 | tf_op jit(solution)/shard_map/ppermute | solution.py:20
  31.0 52.6 %collective-permute-start.1 = (bf16[64,9216]{1,0:T(8,128)(2,1)}, bf16[64,9216]{1,0:T(8,128)(2,1)}, u32[]{:S(2)}, u32[]{:S(2)}) collective-permute-start(bf16[64,9216]{1,0:T(8,128)(2,1)} %all-gather.2.cloned.1.call-done), channel_id=1, source_target_pairs={{4,0},{8,4},{12,8},{16,12},{20,16},{24,20},{28,24},{5,1},{9,5},{13... | collective-permute-start | bytes 3538952 | tf_op jit(solution)/shard_map/ppermute | solution.py:22
  35.2 153.1 %all-to-all-start = ((s32[8,1,16]{2,1,0:T(1,128)}), s32[8,1,16]{2,1,0:T(1,128)S(1)}, u32[]{:S(2)}, u32[]{:S(2)}) async-start(s32[8,1,16]{2,1,0:T(1,128)} %bitcast.3), calls=%async_computation | async-start | bytes 8192 | tf_op jit(solution)/shard_map/all_to_all | solution.py:86
  82.6 1.0 copy-start.2
  93.8 25.1 %copy-start.3 = (bf16[64,48,48,1]{2,1,0,3:T(8,128)(2,1)S(1)}, bf16[64,48,48,1]{2,1,0,3:T(8,128)(2,1)}, u32[]{:S(2)}) copy-start(bf16[64,48,48,1]{2,1,0,3:T(8,128)(2,1)} %reshape.190) | copy-start | bytes 884740
  93.8 25.1 %copy-start.5 = (pred[64,6]{1,0:T(8,128)(4,1)S(1)}, pred[64,6]{1,0:T(8,128)(4,1)}, u32[]{:S(2)}) copy-start(pred[64,6]{1,0:T(8,128)(4,1)} %copy.23) | copy-start | bytes 1156
  135.8 11.4 %copy-start.4 = (s32[64,6]{1,0:T(8,128)S(1)}, s32[64,6]{1,0:T(8,128)}, u32[]{:S(2)}) copy-start(s32[64,6]{1,0:T(8,128)} %copy.26) | copy-start | bytes 4612
  169.7 7.1 %copy-start.6 = (pred[8,16]{1,0:T(8,128)(4,1)S(1)}, pred[8,16]{1,0:T(8,128)(4,1)}, u32[]{:S(2)}) copy-start(pred[8,16]{1,0:T(8,128)(4,1)} %compare_and_fusion.1) | copy-start | bytes 388
  169.7 7.1 %copy-start.7 = (pred[8,16]{1,0:T(8,128)(4,1)S(1)}, pred[8,16]{1,0:T(8,128)(4,1)}, u32[]{:S(2)}) copy-start(pred[8,16]{1,0:T(8,128)(4,1)} %gt.35) | copy-start | bytes 388
  188.4 208.2 %all-to-all-start.1 = ((f32[8,16,48,384]{3,1,2,0:T(8,128)}), f32[8,16,48,384]{3,1,2,0:T(8,128)}, u32[]{:S(2)}, u32[]{:S(2)}) async-start(f32[8,16,48,384]{3,1,2,0:T(8,128)} %fusion.3), calls=%async_computation.1 | async-start | bytes 18874368 | tf_op jit(solution)/shard_map/all_to_all | solution.py:85
  193.5 239.2 %reduce-scatter.2.cloned.1.call-start = ((), (), s32[]{:S(2)}) async-start(), calls=%async_computation.4 | async-start | bytes 1474560 | tf_op jit(solution)/shard_map/reduce_scatter | solution.py:89
  396.6 36.2 %copy-start.1 = (s32[64]{0:T(128)S(1)}, s32[64]{0:T(128)}, u32[]{:S(2)}) copy-start(s32[64]{0:T(128)} %param.11) | copy-start | bytes 772
Sparse Core Ops, SparseCore 0:
  8.9 18.9 all-gather.1
  405.9 26.7 reduce-scatter.1
where the time goes:
time: 443 us; the launch traced here: 440 us
  waiting for transfers between devices  280 us (63%)
  local copies, waits for them, and re-layouts  76.5 us (17%)
  matrix products  32.8 us (7%)
  other arithmetic  19.4 us (4%)
  starting transfers between devices  16.9 us (4%)
  between operations  13.5 us (3%)
    all_to_all x1, waiting for transfers between devices, on_device(): lax.all_to_all(packed, 'wide', split_axis=0, concat_axis=0, tiled=True)  202 us
    gather x2, local copies, waits for them, and re-layouts, on_device(): jnp.take(nearby, local_cols.reshape(-1), axis=0)  33.1 us
    ppermute x1, waiting for transfers between devices, padded(): lax.ppermute(tail, axis, [(i, (i + 1) % count) for i in range(ends)])  32.9 us
    reduce_scatter x1, waiting for transfers between devices, on_device(): lax.psum_scatter(gathered_rows, 'narrow', scatter_dimension=1, tiled=True)  26.9 us
    all_gather x1, waiting for transfers between devices, on_device(): complete = lax.all_gather(prolong, 'narrow', axis=1, tiled=True)  18.2 us
    dot_general x1, matrix products, on_device(): jnp.einsum('irc,ikrm->ikcm', own_rows, applied, preferred_element_type=jn...  16.8 us
    dot_general x1, matrix products, slot_rows(): jnp.einsum('iks,ikcm->icsm', selector, projected, precision=lax.Precision...  11.8 us
    select_n x1, other arithmetic, pack_rows(): packed = jnp.where(value_mask, picked, jnp.zeros_like(picked))  11.6 us
  transfers between devices with their start and end apart: 6, of which 4 were waited for; matrix products, arithmetic and copies ran while one was open for 27% of the time, Pallas kernels for 0%

commit v1 on v0

v1 whole, which is shorter than its diff:
```python
import functools

import jax
import jax.numpy as jnp
from jax import lax
from jax.experimental import pallas as pl
from jax.experimental.pallas import tpu as pltpu
from jax.sharding import PartitionSpec as P

B = 192
M = 48
KC = 8
AGG_DEV = 16
HALF = 64
QUAD = 4
MESH = pl.DeviceIdType.MESH
F32 = jnp.float32
BF16 = jnp.bfloat16
I32 = jnp.int32


def padded(cells, axis):
    count = lax.axis_size(axis)
    ends = count - 1
    return jnp.concatenate(
        [
            lax.ppermute(cells, axis, [(i, (i + 1) % count) for i in range(ends)]),
            cells,
            lax.ppermute(cells, axis, [((i + 1) % count, i) for i in range(ends)]),
        ],
        axis=0,
    )


def product_kernel(terms, parts, col_ref, slot_ref, op_ref, near_ref, own_ref, out_ref, acc):
    step = pl.program_id(0)
    side = M // parts
    lane_half = lax.broadcasted_iota(I32, (M, 2 * HALF), 1) // HALF
    rows = []
    for j in range(QUAD):
        base = (step * QUAD + j) * terms
        acc[j] = jnp.zeros_like(acc[j])
        applied = [
            jnp.dot(op_ref[j, k], near_ref[col_ref[base + k]], preferred_element_type=F32).astype(BF16)
            for k in range(terms)
        ]
        projected = jnp.dot(own_ref[j], jnp.concatenate(applied, axis=1), preferred_element_type=F32)
        for k in range(terms):
            slot = slot_ref[base + k]
            piece = projected[:, k * 2 * HALF : (k + 1) * 2 * HALF]
            acc[j, slot // 2] += jnp.where(lane_half == slot % 2, piece, 0.0)
        rows.append(
            jnp.concatenate(
                [acc[j, s // 2][:, (s % 2) * HALF : (s % 2) * HALF + M] for s in range(KC)], axis=1
            )
        )
    for g in range(parts):
        out_ref[g] = jnp.concatenate([row[g * side : (g + 1) * side] for row in rows], axis=0)


def products(op_blocks, near, own, cols, slots, parts):
    count_rows, terms, part_rows, _ = op_blocks.shape
    side = M // parts
    return pl.pallas_call(
        functools.partial(product_kernel, terms, parts),
        out_shape=jax.ShapeDtypeStruct((parts, count_rows * side, KC * M), F32),
        grid_spec=pltpu.PrefetchScalarGridSpec(
            num_scalar_prefetch=2,
            grid=(count_rows // QUAD,),
            in_specs=[
                pl.BlockSpec((QUAD, terms, part_rows, B), lambda i, *_: (i, 0, 0, 0)),
                pl.BlockSpec(memory_space=pltpu.VMEM),
                pl.BlockSpec((QUAD, M, part_rows), lambda i, *_: (i, 0, 0)),
            ],
            out_specs=pl.BlockSpec((parts, QUAD * side, KC * M), lambda i, *_: (0, i, 0)),
            scratch_shapes=[pltpu.VMEM((QUAD, KC // 2, M, 2 * HALF), F32)],
        ),
        compiler_params=pltpu.CompilerParams(vmem_limit_bytes=48 << 20),
    )(cols, slots, op_blocks, near, own)


def exchange_kernel(
    count, parts, part_ref, src_ref, lab_ref, out_ref,
    rx1, tx2, rx2, pk, rxw, rxl, summed, ns, nr, ws, wr, ls, lr,
):
    wide = lax.axis_index("wide")
    me = lax.axis_index("narrow")
    near = me + 1 - 2 * (me % 2)
    far = (me + 2) % parts
    cross = (near + 2) % parts
    barrier = pltpu.get_barrier_semaphore()
    pl.semaphore_signal(barrier, inc=1, device_id=(wide, near), device_id_type=MESH)
    pl.semaphore_signal(barrier, inc=1, device_id=(wide, far), device_id_type=MESH)

    @pl.loop(1, count)
    def _(d):
        pl.semaphore_signal(barrier, inc=1, device_id=((wide + d) % count, me), device_id_type=MESH)

    pl.semaphore_wait(barrier, count + 1)

    def remote(src, dst, s, r, target):
        return pltpu.make_async_remote_copy(
            src_ref=src, dst_ref=dst, send_sem=s, recv_sem=r, device_id=target, device_id_type=MESH
        )

    first = remote(part_ref.at[cross], rx1.at[1], ns.at[1], nr.at[1], (wide, near))
    second = remote(part_ref.at[near], rx1.at[0], ns.at[0], nr.at[0], (wide, near))
    third = remote(tx2, rx2, ns.at[2], nr.at[2], (wide, far))
    first.start()
    second.start()
    first.wait()
    tx2[...] = (part_ref[far] + rx1[1]).astype(BF16)
    third.start()
    second.wait()
    third.wait()
    summed[...] = (part_ref[me] + rx1[0] + rx2[...].astype(F32)).astype(BF16)

    height = pk.shape[1]
    lanes = lax.broadcasted_iota(I32, (height, summed.shape[0]), 1)

    def send(d):
        other = (wide + d) % count
        return (
            remote(pk.at[d], rxw.at[d], ws.at[d], wr.at[d], (other, me)),
            remote(lab_ref.at[other], rxl.at[d], ls.at[d], lr.at[d], (other, me)),
        )

    def packed(d):
        pick = (src_ref[(wide + d) % count] == lanes).astype(F32).astype(BF16)
        pk[d] = jnp.dot(pick, summed[...], preferred_element_type=F32).astype(BF16)

    @pl.loop(1, count)
    def _(d):
        packed(d)
        for copy in send(d):
            copy.start()

    packed(0)
    places = lax.broadcasted_iota(I32, (out_ref.shape[0], height), 0)

    def placed(labels, rows):
        pick = (labels == places).astype(F32).astype(BF16)
        return jnp.dot(pick, rows, preferred_element_type=F32)

    out_ref[...] = placed(lab_ref[wide], pk[0])

    @pl.loop(1, count)
    def _(d):
        for copy in send(d):
            copy.wait()
        out_ref[...] += placed(rxl[d], rxw[d])


def exchange(part, src, lab, parts, side):
    rows, columns = part.shape[1:]
    count, _, height = lab.shape
    vmem = pl.BlockSpec(memory_space=pltpu.VMEM)
    dma = pltpu.SemaphoreType.DMA
    return pl.pallas_call(
        functools.partial(exchange_kernel, count, parts),
        out_shape=jax.ShapeDtypeStruct((AGG_DEV * side, columns), F32),
        in_specs=[vmem] * 3,
        out_specs=vmem,
        scratch_shapes=[
            pltpu.VMEM((2, rows, columns), F32),
            pltpu.VMEM((rows, columns), BF16),
            pltpu.VMEM((rows, columns), BF16),
            pltpu.VMEM((count, height, columns), BF16),
            pltpu.VMEM((count, height, columns), BF16),
            pltpu.VMEM((count, 1, height), I32),
            pltpu.VMEM((rows, columns), BF16),
            dma((3,)), dma((3,)), dma((count,)), dma((count,)), dma((count,)), dma((count,)),
        ],
        compiler_params=pltpu.CompilerParams(
            collective_id=0, has_side_effects=True, vmem_limit_bytes=48 << 20
        ),
    )(part, src, lab)


def routes(owner, local, count, capacity, side):
    rows = owner.shape[0]
    index = jnp.arange(rows, dtype=I32)
    earlier = (owner[:, None] == owner[None, :]) & (index[None, :] < index[:, None])
    rank = jnp.sum(earlier.astype(I32), axis=1)
    height = -(-capacity * side // 16) * 16
    place = jnp.arange(height, dtype=I32)
    wanted = jnp.arange(count, dtype=I32)[:, None] * capacity + place[None, :] // side
    wanted = jnp.where(place[None, :] < capacity * side, wanted, -1)
    match = wanted[:, :, None] == (owner * capacity + rank)[None, None, :]
    filled = jnp.any(match, axis=2)
    inner = place[None, :] % side

    def spread(values):
        picked = jnp.sum(jnp.where(match, values[None, None, :], 0), axis=2)
        return jnp.where(filled, picked * side + inner, -1)

    return spread(index)[:, :, None], spread(local)[:, None, :]


def on_device(op_blocks, prolong, col_index, slot_index, dest_owner, dest_local):
    count_rows, _, part_rows, _ = op_blocks.shape
    count = lax.axis_size("wide")
    parts = lax.axis_size("narrow")
    wide_pos = lax.axis_index("wide")
    capacity = max(2, 2 * count_rows // count)
    side = M // parts
    src, lab = routes(dest_owner[:, 0], dest_local, count, capacity, side)
    complete = lax.all_gather(prolong, "narrow", axis=1, tiled=True)
    nearby = padded(complete, "wide").reshape(3 * count_rows, B, M)
    gap = jnp.zeros((3 * count_rows, B, HALF - M), BF16)
    near = jnp.concatenate([nearby, gap, nearby, gap], axis=2)
    cols = col_index - wide_pos * count_rows + count_rows
    own = prolong.reshape(count_rows, part_rows, M).swapaxes(1, 2)
    part = products(op_blocks, near, own, cols.reshape(-1), slot_index.reshape(-1), parts)
    coarse = exchange(part, src, lab, parts, side)
    return coarse.reshape(AGG_DEV, side, KC * M)


def solution(mesh):
    in_specs = (
        P("wide", None, "narrow", None),
        P("wide", "narrow"),
        P("wide", None),
        P("wide", None),
        P("wide", None),
        P("wide"),
    )
    out_specs = P("wide", "narrow", None)
    return jax.shard_map(
        on_device, mesh=mesh, in_specs=in_specs, out_specs=out_specs, check_vma=False
    )
```

time: 443 us -> 222 us (0.50)
  waiting for transfers between devices: 280 us -> 65 us
  Pallas kernels: 0 us -> 74.6 us
  local copies, waits for them, and re-layouts: 76.5 us -> 35.9 us
  matrix products: 32.8 us -> 0 us
  starting transfers between devices: 16.9 us -> 6.19 us
  other arithmetic: 19.4 us -> 26.4 us
    all_to_all x2 -> x0, waiting for transfers between devices: 202 us -> none  [the longest x1 202 us: on_device(): lax.all_to_all(packed, 'wide', split_axis=0, concat_axis=0, tiled=True)]
    pallas_call x0 -> x2, Pallas kernels: none -> 74.6 us  [the longest x1 51.1 us: exchange(): pl.pallas_call(functools.partial(exchange_kernel, count, parts), out_shap...]
    gather x5 -> x0, local copies, waits for them, and re-layouts: 41.5 us -> none  [the longest x2 33.1 us: on_device(): jnp.take(nearby, local_cols.reshape(-1), axis=0)]
    dot_general x3 -> x0, matrix products: 32.8 us -> none  [the longest x1 16.8 us: on_device(): jnp.einsum('irc,ikrm->ikcm', own_rows, applied, preferred_element_type=jn...]
    reduce_scatter x1 -> x0, waiting for transfers between devices: 26.9 us -> none  [on_device(): lax.psum_scatter(gathered_rows, 'narrow', scatter_dimension=1, tiled=True)]
    concatenate x1 -> x2, other arithmetic: 2.16 us -> 23 us  [the longest x1 17.4 us: on_device(): near = jnp.concatenate([nearby, gap, nearby, gap], axis=2)]
    select_n x4 -> x5, other arithmetic: 12.2 us -> 0.11 us  [the longest x1 0.07 us: routes(): wanted = jnp.where(place[None, :] < capacity * side, wanted, -1)]
    all_to_all x2 -> x0, starting transfers between devices: 11.7 us -> none  [the longest x1 6.51 us: on_device(): lax.all_to_all(labels, 'wide', split_axis=0, concat_axis=0, tiled=True)]
  transfers between devices with their start and end apart: 6 -> 3, of which waited for: 4 -> 2; matrix products, arithmetic and copies ran while one was open for 27% -> 5% of each run, Pallas kernels for 0% -> 0%
where the time goes in v1:
time: 222 us
  Pallas kernels  74.6 us (34%)
  waiting for transfers between devices  65 us (29%)
  local copies, waits for them, and re-layouts  35.9 us (16%)
  other arithmetic  26.4 us (12%)
  between operations  13.5 us (6%)
  starting transfers between devices  6.19 us (3%)
    pallas_call x1, Pallas kernels, exchange(): pl.pallas_call(functools.partial(exchange_kernel, count, parts), out_shap...  51.1 us
    ppermute x1, waiting for transfers between devices, padded(): lax.ppermute(cells, axis, [((i + 1) % count, i) for i in range(ends)])  41.3 us
    all_gather x1, waiting for transfers between devices, on_device(): complete = lax.all_gather(prolong, 'narrow', axis=1, tiled=True)  23.6 us
    pallas_call x1, Pallas kernels, products(): pl.pallas_call(functools.partial(product_kernel, terms, parts), out_shape...  23.5 us
    concatenate x1, other arithmetic, on_device(): near = jnp.concatenate([nearby, gap, nearby, gap], axis=2)  17.4 us
    reshape x1, local copies, waits for them, and re-layouts, on_device(): nearby = padded(complete, 'wide').reshape(3 * count_rows, B, M)  12.9 us
    broadcast_in_dim x1, local copies, waits for them, and re-layouts, on_device(): gap = jnp.zeros((3 * count_rows, B, HALF - M), BF16)  6 us
    concatenate x1, other arithmetic, padded(): jnp.concatenate([lax.ppermute(cells, axis, [(i, (i + 1) % count) for i in...  5.65 us
  transfers between devices with their start and end apart: 3, of which 2 were waited for; matrix products, arithmetic and copies ran while one was open for 5% of the time, Pallas kernels for 0%

profile of v1, /device:TPU:13, one launch (start us, length us, event | category | flops | bytes accessed | tf_op | source)
XLA Modules:
  0.0 221.6 jit_solution(3714589759593143670)
XLA Ops:
  6.5 0.0 all-gather.2.cloned.1.call-start
  6.5 2.0 copy.46
  8.5 0.0 all-gather.2.cloned.1.call-update
  8.6 0.9 convert_reduce_fusion
  9.5 0.7 multiply_add_fusion
  10.2 0.7 subtract_add_fusion
  10.9 23.6 %all-gather.2.cloned.1.call-done = bf16[64,9216]{0,1:T(8,128)(2,1)} async-done(((bf16[64,2304]{0,1:T(8,128)(2,1)}), bf16[64,9216]{0,1:T(8,128)(2,1)}) %all-gather.2.cloned.1.call-update) | async-done | bytes 1179664 | tf_op jit(solution)/shard_map/all_gather | solution.py:208
  34.5 2.8 %copy.47 = bf16[64,9216]{1,0:T(8,128)(2,1)S(1)} copy(bf16[64,9216]{0,1:T(8,128)(2,1)} %all-gather.2.cloned.1.call-done) | data formatting | bytes 2359296 | tf_op jit(solution)/shard_map/all_gather | solution.py:208
  37.3 2.2 collective-permute-start.1
  39.5 4.0 %collective-permute-start = (bf16[64,9216]{1,0:T(8,128)(2,1)S(1)}, bf16[64,9216]{1,0:T(8,128)(2,1)}, u32[]{:S(2)}, u32[]{:S(2)}) collective-permute-start(bf16[64,9216]{1,0:T(8,128)(2,1)S(1)} %copy.47), channel_id=1, source_target_pairs={{0,4},{4,8},{8,12},{12,16},{16,20},{20,24},{24,28},{1,5},{5,9},{9,... | collective-permute-start | bytes 3538952 | tf_op jit(solution)/shard_map/ppermute | solution.py:27
  43.6 2.0 reshape.188
  45.6 0.1 copy.44
  45.7 0.1 reshape.185.col_ref
  45.8 0.8 copy.45
  46.6 0.1 reshape.186.slot_ref
  46.7 0.4 copy.53
  47.1 0.1 add_select_fusion
  47.2 0.1 compare_reduce_fusion
  47.3 0.9 fusion.1
  48.2 0.3 copy.55.src_ref
  48.6 41.3 %collective-permute-done.1 = bf16[64,9216]{1,0:T(8,128)(2,1)} collective-permute-done((bf16[64,9216]{1,0:T(8,128)(2,1)S(1)}, bf16[64,9216]{1,0:T(8,128)(2,1)}, u32[]{:S(2)}, u32[]{:S(2)}) %collective-permute-start.1) | collective-permute-done | bytes 1179680 | tf_op jit(solution)/shard_map/ppermute | solution.py:29
  89.9 3.8 %copy.50 = bf16[64,9216]{0,1:T(8,128)(2,1)} copy(bf16[64,9216]{1,0:T(8,128)(2,1)} %collective-permute-done.1) | data formatting | bytes 2359296 | tf_op jit(solution)/shard_map/ppermute | solution.py:29
  93.7 0.0 collective-permute-done
  93.7 3.7 %copy.49 = bf16[64,9216]{0,1:T(8,128)(2,1)} copy(bf16[64,9216]{1,0:T(8,128)(2,1)} %collective-permute-done) | data formatting | bytes 2359296 | tf_op jit(solution)/shard_map/ppermute | solution.py:27
  97.4 5.6 %pad_maximum_fusion.1 = bf16[192,9216]{0,1:T(8,128)(2,1)} fusion(bf16[64,9216]{0,1:T(8,128)(2,1)} %copy.50, bf16[64,9216]{0,1:T(8,128)(2,1)} %all-gather.2.cloned.1.call-done, bf16[64,9216]{0,1:T(8,128)(2,1)} %copy.49), kind=kLoop, calls=%fused_computation.1 | loop fusion | flops 10616832 | bytes 7077888 | tf_op jit(solution)/shard_map/concatenate | solution.py:25
  103.0 12.9 %copy.51 = bf16[192,192,48]{2,1,0:T(8,128)(2,1)} copy(bf16[192,192,48]{0,2,1:T(8,128)(2,1)} %bitcast.12) | data formatting | bytes 7077888 | tf_op jit(solution)/shard_map/reshape | solution.py:209
  116.0 6.0 %broadcast_in_dim.52 = bf16[192,192,16]{2,1,0:T(8,128)(2,1)} broadcast(bf16[]{:T(256)} %constant.17.clone.1), dimensions={} | broadcast | bytes 1179650 | tf_op jit(solution)/shard_map/broadcast_in_dim | solution.py:210
  122.0 0.0 copy-done
  122.0 17.4 %pad_maximum_fusion.near_ref = bf16[192,192,128]{2,1,0:T(8,128)(2,1)} fusion(bf16[192,192,16]{2,1,0:T(8,128)(2,1)} %broadcast_in_dim.52, bf16[192,192,48]{2,1,0:T(8,128)(2,1)S(1)} %copy-done), kind=kLoop, calls=%fused_computation | loop fusion | flops 37748736 | bytes 14155776 | tf_op jit(solution)/shard_map/concatenate | solution.py:211
  139.3 23.5 %shard_map.64.part_ref = f32[4,768,384]{2,1,0:T(8,128)S(1)} custom-call(s32[384]{0:T(512)S(1)} %reshape.185.col_ref, s32[384]{0:T(512)S(1)} %reshape.186.slot_ref, bf16[64,6,48,192]{3,2,1,0:T(8,128)(2,1)} %op_ref.1, bf16[192,192,128]{2,1,0:T(8,128)(2,1)} %pad_maximum_fusion.near_ref, bf16[64,48,48]{2,1,0:T(8,128)(2,1)S(1)} %bitcast.11), custom_call_target="tpu_custom_call" | custom-call | tf_op jit(solution)/shard_map/pallas_call | solution.py:64
  162.8 51.1 %shard_map.65 = f32[192,384]{1,0:T(8,128)S(1)} custom-call(f32[4,768,384]{2,1,0:T(8,128)S(1)} %shard_map.64.part_ref, s32[8,192,1]{2,1,0:T(8,128)S(1)} %copy.55.src_ref, s32[8,1,192]{2,1,0:T(1,128)S(1)} %copy_select_fusion.lab_ref), custom_call_target="tpu_custom_call" | custom-call | tf_op jit(solution)/shard_map/pallas_call | solution.py:159
  214.0 0.8 copy.56
  (9 shorter events, 0.1 us)
Async XLA Ops:
  6.5 28.0 %all-gather.2.cloned.1.call-start = ((), (), s32[]{:S(2)}) async-start(), calls=%async_computation | async-start | bytes 2949120 | tf_op jit(solution)/shard_map/all_gather | solution.py:208
  37.3 52.5 %collective-permute-start.1 = (bf16[64,9216]{1,0:T(8,128)(2,1)S(1)}, bf16[64,9216]{1,0:T(8,128)(2,1)}, u32[]{:S(2)}, u32[]{:S(2)}) collective-permute-start(bf16[64,9216]{1,0:T(8,128)(2,1)S(1)} %copy.47), channel_id=1, source_target_pairs={{4,0},{8,4},{12,8},{16,12},{20,16},{24,20},{28,24},{5,1},{9,5},{13... | collective-permute-start | bytes 3538952 | tf_op jit(solution)/shard_map/ppermute | solution.py:29
  39.5 54.1 %collective-permute-start = (bf16[64,9216]{1,0:T(8,128)(2,1)S(1)}, bf16[64,9216]{1,0:T(8,128)(2,1)}, u32[]{:S(2)}, u32[]{:S(2)}) collective-permute-start(bf16[64,9216]{1,0:T(8,128)(2,1)S(1)} %copy.47), channel_id=1, source_target_pairs={{0,4},{4,8},{8,12},{12,16},{16,20},{20,24},{24,28},{1,5},{5,9},{9,... | collective-permute-start | bytes 3538952 | tf_op jit(solution)/shard_map/ppermute | solution.py:27
  116.0 6.0 %copy-start = (bf16[192,192,48]{2,1,0:T(8,128)(2,1)S(1)}, bf16[192,192,48]{2,1,0:T(8,128)(2,1)}, u32[]{:S(2)}) copy-start(bf16[192,192,48]{2,1,0:T(8,128)(2,1)} %copy.51) | copy-start | bytes 10616836
Sparse Core Ops, SparseCore 0:
  8.9 25.5 all-gather.1

commit v2 on v1

--- a/solution.py
+++ b/solution.py
@@ -19,20 +19,118 @@
 I32 = jnp.int32
 
 
-def padded(cells, axis):
-    count = lax.axis_size(axis)
-    ends = count - 1
-    return jnp.concatenate(
-        [
-            lax.ppermute(cells, axis, [(i, (i + 1) % count) for i in range(ends)]),
-            cells,
-            lax.ppermute(cells, axis, [((i + 1) % count, i) for i in range(ends)]),
-        ],
-        axis=0,
+def gather_kernel(count, parts, chunks, own_ref, near_ref, ss, rs, keep_sem):
+    wide = lax.axis_index("wide")
+    me = lax.axis_index("narrow")
+    near = me + 1 - 2 * (me % 2)
+    far = (me + 2) % parts
+    pairs, depth, _ = own_ref.shape
+    piece = pairs // chunks
+    first, last = wide == 0, wide == count - 1
+    has = {0: jnp.logical_not(first), 1: None, 2: jnp.logical_not(last)}
+    barrier = pltpu.get_barrier_semaphore()
+
+    def when(cond, fn):
+        fn() if cond is None else pl.when(cond)(fn)
+
+    def hello(where):
+        pl.semaphore_signal(barrier, inc=1, device_id=where, device_id_type=MESH)
+
+    hello((wide, near))
+    hello((wide, far))
+    when(has[0], lambda: hello((wide - 1, me)))
+    when(has[2], lambda: hello((wide + 1, me)))
+    sides = (wide + count - 1) // count + (2 * count - 2 - wide) // count
+    pl.semaphore_wait(barrier, 2 + sides)
+
+    def place(slot, part, c):
+        return near_ref.at[pl.ds(slot * pairs + c * piece, piece), pl.ds(part * depth, depth)]
+
+    def remote(slot, kind, c, target, source, part):
+        return pltpu.make_async_remote_copy(
+            src_ref=source,
+            dst_ref=place(slot, part, c),
+            send_sem=ss.at[slot, kind, c],
+            recv_sem=rs.at[slot, kind, c],
+            device_id=target,
+            device_id_type=MESH,
+        )
+
+    def mine(c):
+        return own_ref.at[pl.ds(c * piece, piece)]
+
+    def direct(slot, c):
+        target = (wide + 1 if slot == 0 else wide - 1, me)
+        return remote(slot, 0, c, target, mine(c), me)
+
+    def held(slot, c):
+        return mine(c) if slot == 1 else place(slot, me, c)
+
+    def to_near(slot, c):
+        return remote(slot, 1, c, (wide, near), held(slot, c), me)
+
+    def to_far(slot, c):
+        return remote(slot, 2, c, (wide, far), held(slot, c), me)
+
+    def onward(slot, c):
+        return remote(slot, 3, c, (wide, near), place(slot, far, c), far)
+
+    keep = pltpu.make_async_copy(
+        own_ref, near_ref.at[pl.ds(pairs, pairs), pl.ds(me * depth, depth)], keep_sem
     )
-
-
-def product_kernel(terms, parts, col_ref, slot_ref, op_ref, near_ref, own_ref, out_ref, acc):
+    for c in range(chunks):
+        to_far(1, c).start()
+        when(has[2], lambda: direct(0, c).start())
+        when(has[0], lambda: direct(2, c).start())
+        to_near(1, c).start()
+    keep.start()
+
+    def spread(slot, c):
+        direct(slot, c).wait_recv()
+        to_far(slot, c).start()
+        to_near(slot, c).start()
+
+    def forward(slot, c):
+        to_far(slot, c).wait_recv()
+        onward(slot, c).start()
+
+    for c in range(chunks):
+        forward(1, c)
+        when(has[0], lambda: spread(0, c))
+        when(has[2], lambda: spread(2, c))
+    for c in range(chunks):
+        when(has[0], lambda: forward(0, c))
+        when(has[2], lambda: forward(2, c))
+
+    def drain(slot):
+        for c in range(chunks):
+            to_near(slot, c).wait()
+            to_far(slot, c).wait_send()
+            onward(slot, c).wait()
+
+    for slot in range(3):
+        when(has[slot], lambda: drain(slot))
+    for c in range(chunks):
+        when(has[2], lambda: direct(0, c).wait_send())
+        when(has[0], lambda: direct(2, c).wait_send())
+    keep.wait()
+
+
+def gathered(own, count, parts, chunks=4):
+    pairs, depth, lanes = own.shape
+    hbm = pl.BlockSpec(memory_space=pl.ANY)
+    sems = pltpu.SemaphoreType.DMA((3, 4, chunks))
+    return pl.pallas_call(
+        functools.partial(gather_kernel, count, parts, chunks),
+        out_shape=jax.ShapeDtypeStruct((3 * pairs, parts * depth, lanes), BF16),
+        in_specs=[hbm],
+        out_specs=hbm,
+        scratch_shapes=[sems, sems, pltpu.SemaphoreType.DMA],
+        compiler_params=pltpu.CompilerParams(collective_id=1, has_side_effects=True),
+    )(own)
+
+
+def product_kernel(terms, parts, tile_ref, swap_ref, slot_ref, op_ref, near_ref, own_ref, out_ref, acc):
     step = pl.program_id(0)
     side = M // parts
     lane_half = lax.broadcasted_iota(I32, (M, 2 * HALF), 1) // HALF
@@ -41,13 +139,14 @@
         base = (step * QUAD + j) * terms
         acc[j] = jnp.zeros_like(acc[j])
         applied = [
-            jnp.dot(op_ref[j, k], near_ref[col_ref[base + k]], preferred_element_type=F32).astype(BF16)
+            jnp.dot(op_ref[j, k], near_ref[tile_ref[base + k]], preferred_element_type=F32).astype(BF16)
             for k in range(terms)
         ]
         projected = jnp.dot(own_ref[j], jnp.concatenate(applied, axis=1), preferred_element_type=F32)
         for k in range(terms):
             slot = slot_ref[base + k]
             piece = projected[:, k * 2 * HALF : (k + 1) * 2 * HALF]
+            piece = jnp.where(swap_ref[base + k] == 1, pltpu.roll(piece, HALF, 1), piece)
             acc[j, slot // 2] += jnp.where(lane_half == slot % 2, piece, 0.0)
         rows.append(
             jnp.concatenate(
@@ -58,14 +157,14 @@
         out_ref[g] = jnp.concatenate([row[g * side : (g + 1) * side] for row in rows], axis=0)
 
 
-def products(op_blocks, near, own, cols, slots, parts):
+def products(op_blocks, near, own, tiles, swaps, slots, parts):
     count_rows, terms, part_rows, _ = op_blocks.shape
     side = M // parts
     return pl.pallas_call(
         functools.partial(product_kernel, terms, parts),
         out_shape=jax.ShapeDtypeStruct((parts, count_rows * side, KC * M), F32),
         grid_spec=pltpu.PrefetchScalarGridSpec(
-            num_scalar_prefetch=2,
+            num_scalar_prefetch=3,
             grid=(count_rows // QUAD,),
             in_specs=[
                 pl.BlockSpec((QUAD, terms, part_rows, B), lambda i, *_: (i, 0, 0, 0)),
@@ -76,7 +175,7 @@
             scratch_shapes=[pltpu.VMEM((QUAD, KC // 2, M, 2 * HALF), F32)],
         ),
         compiler_params=pltpu.CompilerParams(vmem_limit_bytes=48 << 20),
-    )(cols, slots, op_blocks, near, own)
+    )(tiles, swaps, slots, op_blocks, near, own)
 
 
 def exchange_kernel(
@@ -205,13 +304,17 @@
     capacity = max(2, 2 * count_rows // count)
     side = M // parts
     src, lab = routes(dest_owner[:, 0], dest_local, count, capacity, side)
-    complete = lax.all_gather(prolong, "narrow", axis=1, tiled=True)
-    nearby = padded(complete, "wide").reshape(3 * count_rows, B, M)
-    gap = jnp.zeros((3 * count_rows, B, HALF - M), BF16)
-    near = jnp.concatenate([nearby, gap, nearby, gap], axis=2)
-    cols = col_index - wide_pos * count_rows + count_rows
-    own = prolong.reshape(count_rows, part_rows, M).swapaxes(1, 2)
-    part = products(op_blocks, near, own, cols.reshape(-1), slot_index.reshape(-1), parts)
+    pairs = count_rows // 2
+    blocks = prolong.reshape(count_rows, part_rows, M)
+    gap = jnp.zeros((pairs, part_rows, HALF - M), BF16)
+    paired = jnp.concatenate([blocks[:pairs], gap, blocks[pairs:], gap], axis=2)
+    near = gathered(paired, count, parts)
+    cols = (col_index - wide_pos * count_rows + count_rows).reshape(-1)
+    slots = slot_index.reshape(-1)
+    inner = cols % count_rows
+    tiles = cols // count_rows * pairs + inner % pairs
+    swaps = (inner // pairs + slots) % 2
+    part = products(op_blocks, near, blocks.swapaxes(1, 2), tiles, swaps, slots, parts)
     coarse = exchange(part, src, lab, parts, side)
     return coarse.reshape(AGG_DEV, side, KC * M)
 

time: 222 us -> 118 us (0.53)
  waiting for transfers between devices: 65 us -> 0 us
  Pallas kernels: 74.6 us -> 106 us
  local copies, waits for them, and re-layouts: 35.9 us -> 9.72 us
  other arithmetic: 26.4 us -> 1.93 us
  between operations: 13.5 us -> 0.21 us
  starting transfers between devices: 6.19 us -> 0 us
    ppermute x2 -> x0, waiting for transfers between devices: 41.3 us -> none  [the longest x1 41.3 us: padded(): lax.ppermute(cells, axis, [((i + 1) % count, i) for i in range(ends)])]
    pallas_call x0 -> x1, Pallas kernels: none -> 34.5 us  [gathered(): pl.pallas_call(functools.partial(gather_kernel, count, parts, chunks), ou...]
    all_gather x1 -> x0, waiting for transfers between devices: 23.6 us -> none  [on_device(): complete = lax.all_gather(prolong, 'narrow', axis=1, tiled=True)]
    concatenate x2 -> x1, other arithmetic: 23 us -> 1.23 us  [on_device(): paired = jnp.concatenate([blocks[:pairs], gap, blocks[pairs:], gap], axis=2)]
    reshape x5 -> x4, local copies, waits for them, and re-layouts: 15.6 us -> 1.72 us  [the longest x2 1.44 us: on_device(): blocks = prolong.reshape(count_rows, part_rows, M)]
    ppermute x2 -> x0, local copies, waits for them, and re-layouts: 7.49 us -> none  [the longest x1 3.78 us: padded(): lax.ppermute(cells, axis, [((i + 1) % count, i) for i in range(ends)])]
    ppermute x2 -> x0, starting transfers between devices: 6.18 us -> none  [the longest x1 4 us: padded(): lax.ppermute(cells, axis, [(i, (i + 1) % count) for i in range(ends)])]
    broadcast_in_dim x1, local copies, waits for them, and re-layouts: 6 us -> 0.05 us  [on_device(): gap = jnp.zeros((pairs, part_rows, HALF - M), BF16)]
  transfers between devices with their start and end apart: 3 -> 0, of which waited for: 2 -> 0; matrix products, arithmetic and copies ran while one was open for 5% -> 0% of each run, Pallas kernels for 0% -> 0%
where the time goes in v2:
time: 118 us
  Pallas kernels  106 us (90%)
  local copies, waits for them, and re-layouts  9.72 us (8%)
  other arithmetic  1.93 us (2%)
    pallas_call x1, Pallas kernels, exchange(): pl.pallas_call(functools.partial(exchange_kernel, count, parts), out_shap...  48 us
    pallas_call x1, Pallas kernels, gathered(): pl.pallas_call(functools.partial(gather_kernel, count, parts, chunks), ou...  34.5 us
    pallas_call x1, Pallas kernels, products(): pl.pallas_call(functools.partial(product_kernel, terms, parts), out_shape...  23.2 us
    unnamed x15, local copies, waits for them, and re-layouts  4.57 us

profile of v2, /device:TPU:13, one launch (start us, length us, event | category | flops | bytes accessed | tf_op | source)
XLA Modules:
  0.0 117.6 jit_solution(15622298754231810281)
XLA Ops:
  0.0 0.0 copy-start.2
  0.0 1.0 fusion.12
  1.1 0.6 slice.13
  1.6 0.6 slice.15
  2.2 0.1 broadcast_in_dim.52
  2.2 1.2 %pad_maximum_fusion.own_ref = bf16[32,48,128]{2,1,0:T(8,128)(2,1)} fusion(bf16[32,48,16]{2,1,0:T(8,128)(2,1)S(1)} %broadcast_in_dim.52, bf16[32,48,48]{2,1,0:T(8,128)(2,1)S(1)} %slice.15, bf16[32,48,48]{2,1,0:T(8,128)(2,1)S(1)} %slice.13), kind=kLoop, calls=%fused_computation.5 | loop fusion | flops 1572864 | bytes 737280 | tf_op jit(solution)/shard_map/concatenate | solution.py:310
  3.5 34.5 %shard_map.64.near_ref = bf16[96,192,128]{2,1,0:T(8,128)(2,1)} custom-call(bf16[32,48,128]{2,1,0:T(8,128)(2,1)} %pad_maximum_fusion.own_ref), custom_call_target="tpu_custom_call" | custom-call | tf_op jit(solution)/shard_map/pallas_call | solution.py:123
  38.0 0.0 copy-done.3
  38.0 0.1 copy.22
  38.1 0.1 reshape.185.slot_ref
  38.2 0.0 copy-done.4
  38.2 0.1 copy.21
  38.3 0.1 reshape.184
  38.5 0.0 copy-done.2
  38.5 1.1 reshape.186
  39.6 0.4 copy.23
  40.0 0.0 copy-start.6
  40.0 0.0 copy-start.5
  40.0 23.2 %shard_map.65.part_ref = f32[4,768,384]{2,1,0:T(8,128)S(1)} custom-call(s32[384]{0:T(512)S(1)} %get-tuple-element.10.tile_ref, s32[384]{0:T(512)S(1)} %get-tuple-element.9.swap_ref, s32[384]{0:T(512)S(1)} %reshape.185.slot_ref, bf16[64,6,48,192]{3,2,1,0:T(8,128)(2,1)} %op_ref.1, bf16[96,192,128]{2,1,0:T(8,128)(2,1)} %shard_map.64.near_ref, ...), custom_call_target="tpu_custom_call" | custom-call | tf_op jit(solution)/shard_map/pallas_call | solution.py:163
  63.2 0.0 copy-start
  63.2 2.1 %copy-done = f32[4,768,384]{2,1,0:T(8,128)} copy-done((f32[4,768,384]{2,1,0:T(8,128)}, f32[4,768,384]{2,1,0:T(8,128)S(1)}, u32[]{:S(2)}) %copy-start) | copy-done | bytes 4718616
  65.4 0.1 add_select_fusion
  65.5 0.0 copy-done.6
  65.5 0.2 convert_reduce_fusion
  65.6 0.0 copy-done.5
  65.7 0.2 fusion.1
  65.9 0.1 compare_reduce_fusion
  66.0 0.3 copy.25.src_ref
  66.4 0.0 copy-start.1
  66.4 2.3 %copy-done.1 = f32[4,768,384]{2,1,0:T(8,128)S(1)} copy-done((f32[4,768,384]{2,1,0:T(8,128)S(1)}, f32[4,768,384]{2,1,0:T(8,128)}, u32[]{:S(2)}) %copy-start.1) | copy-done | bytes 4718616
  68.7 48.0 %shard_map.66 = f32[192,384]{1,0:T(8,128)S(1)} custom-call(f32[4,768,384]{2,1,0:T(8,128)S(1)} %copy-done.1, s32[8,192,1]{2,1,0:T(8,128)S(1)} %copy.25.src_ref, s32[8,1,192]{2,1,0:T(1,128)S(1)} %copy_select_fusion.lab_ref), custom_call_target="tpu_custom_call" | custom-call | tf_op jit(solution)/shard_map/pallas_call | solution.py:258
  116.8 0.8 copy.26
  (13 shorter events, 0.1 us)
Async XLA Ops:
  0.0 38.5 %copy-start.2 = (bf16[64,2304]{1,0:T(8,128)(2,1)S(1)}, bf16[64,2304]{1,0:T(8,128)(2,1)}, u32[]{:S(2)}) copy-start(bf16[64,2304]{1,0:T(8,128)(2,1)} %param.7) | copy-start | bytes 884740
  0.0 38.0 %copy-start.3 = (s32[64,6]{0,1:T(8,128)S(1)}, s32[64,6]{0,1:T(8,128)}, u32[]{:S(2)}) copy-start(s32[64,6]{0,1:T(8,128)} %param.9) | copy-start | bytes 4612
  0.0 38.2 %copy-start.4 = (s32[64,6]{0,1:T(8,128)S(1)}, s32[64,6]{0,1:T(8,128)}, u32[]{:S(2)}) copy-start(s32[64,6]{0,1:T(8,128)} %param.8) | copy-start | bytes 4612
  40.0 25.5 %copy-start.6 = (s32[64,1]{0,1:T(1,128)S(1)}, s32[64,1]{0,1:T(1,128)}, u32[]{:S(2)}) copy-start(s32[64,1]{0,1:T(1,128)} %param.10) | copy-start | bytes 772
  40.0 25.7 %copy-start.5 = (s32[64]{0:T(128)S(1)}, s32[64]{0:T(128)}, u32[]{:S(2)}) copy-start(s32[64]{0:T(128)} %param.11) | copy-start | bytes 772
  63.2 2.1 %copy-start = (f32[4,768,384]{2,1,0:T(8,128)}, f32[4,768,384]{2,1,0:T(8,128)S(1)}, u32[]{:S(2)}) copy-start(f32[4,768,384]{2,1,0:T(8,128)S(1)} %shard_map.65.part_ref) | copy-start | bytes 14155780
  66.4 2.3 %copy-start.1 = (f32[4,768,384]{2,1,0:T(8,128)S(1)}, f32[4,768,384]{2,1,0:T(8,128)}, u32[]{:S(2)}) copy-start(f32[4,768,384]{2,1,0:T(8,128)} %copy-done) | copy-start | bytes 14155780

commit v3 on v2

--- a/solution.py
+++ b/solution.py
@@ -130,92 +130,53 @@
     )(own)
 
 
-def product_kernel(terms, parts, tile_ref, swap_ref, slot_ref, op_ref, near_ref, own_ref, out_ref, acc):
+def coarse_kernel(
+    count, parts, terms, steps, chunks,
+    tile_ref, swap_ref, slot_ref, op_ref, near_ref, own_ref, src_ref, lab_ref, out_ref,
+    part, rx1, tx2, rx2, pk, rxw, rxl, summed, ns, nr, ws, wr, ls, lr,
+):
     step = pl.program_id(0)
-    side = M // parts
-    lane_half = lax.broadcasted_iota(I32, (M, 2 * HALF), 1) // HALF
-    rows = []
-    for j in range(QUAD):
-        base = (step * QUAD + j) * terms
-        acc[j] = jnp.zeros_like(acc[j])
-        applied = [
-            jnp.dot(op_ref[j, k], near_ref[tile_ref[base + k]], preferred_element_type=F32).astype(BF16)
-            for k in range(terms)
-        ]
-        projected = jnp.dot(own_ref[j], jnp.concatenate(applied, axis=1), preferred_element_type=F32)
-        for k in range(terms):
-            slot = slot_ref[base + k]
-            piece = projected[:, k * 2 * HALF : (k + 1) * 2 * HALF]
-            piece = jnp.where(swap_ref[base + k] == 1, pltpu.roll(piece, HALF, 1), piece)
-            acc[j, slot // 2] += jnp.where(lane_half == slot % 2, piece, 0.0)
-        rows.append(
-            jnp.concatenate(
-                [acc[j, s // 2][:, (s % 2) * HALF : (s % 2) * HALF + M] for s in range(KC)], axis=1
-            )
-        )
-    for g in range(parts):
-        out_ref[g] = jnp.concatenate([row[g * side : (g + 1) * side] for row in rows], axis=0)
-
-
-def products(op_blocks, near, own, tiles, swaps, slots, parts):
-    count_rows, terms, part_rows, _ = op_blocks.shape
-    side = M // parts
-    return pl.pallas_call(
-        functools.partial(product_kernel, terms, parts),
-        out_shape=jax.ShapeDtypeStruct((parts, count_rows * side, KC * M), F32),
-        grid_spec=pltpu.PrefetchScalarGridSpec(
-            num_scalar_prefetch=3,
-            grid=(count_rows // QUAD,),
-            in_specs=[
-                pl.BlockSpec((QUAD, terms, part_rows, B), lambda i, *_: (i, 0, 0, 0)),
-                pl.BlockSpec(memory_space=pltpu.VMEM),
-                pl.BlockSpec((QUAD, M, part_rows), lambda i, *_: (i, 0, 0)),
-            ],
-            out_specs=pl.BlockSpec((parts, QUAD * side, KC * M), lambda i, *_: (0, i, 0)),
-            scratch_shapes=[pltpu.VMEM((QUAD, KC // 2, M, 2 * HALF), F32)],
-        ),
-        compiler_params=pltpu.CompilerParams(vmem_limit_bytes=48 << 20),
-    )(tiles, swaps, slots, op_blocks, near, own)
-
-
-def exchange_kernel(
-    count, parts, part_ref, src_ref, lab_ref, out_ref,
-    rx1, tx2, rx2, pk, rxw, rxl, summed, ns, nr, ws, wr, ls, lr,
-):
     wide = lax.axis_index("wide")
     me = lax.axis_index("narrow")
     near = me + 1 - 2 * (me % 2)
     far = (me + 2) % parts
     cross = (near + 2) % parts
-    barrier = pltpu.get_barrier_semaphore()
-    pl.semaphore_signal(barrier, inc=1, device_id=(wide, near), device_id_type=MESH)
-    pl.semaphore_signal(barrier, inc=1, device_id=(wide, far), device_id_type=MESH)
-
-    @pl.loop(1, count)
-    def _(d):
-        pl.semaphore_signal(barrier, inc=1, device_id=((wide + d) % count, me), device_id_type=MESH)
-
-    pl.semaphore_wait(barrier, count + 1)
+    side = M // parts
+    per = steps // chunks
+    height = pk.shape[1]
+    chunk_rows = summed.shape[0] // chunks
 
     def remote(src, dst, s, r, target):
         return pltpu.make_async_remote_copy(
             src_ref=src, dst_ref=dst, send_sem=s, recv_sem=r, device_id=target, device_id_type=MESH
         )
 
-    first = remote(part_ref.at[cross], rx1.at[1], ns.at[1], nr.at[1], (wide, near))
-    second = remote(part_ref.at[near], rx1.at[0], ns.at[0], nr.at[0], (wide, near))
-    third = remote(tx2, rx2, ns.at[2], nr.at[2], (wide, far))
-    first.start()
-    second.start()
-    first.wait()
-    tx2[...] = (part_ref[far] + rx1[1]).astype(BF16)
-    third.start()
-    second.wait()
-    third.wait()
-    summed[...] = (part_ref[me] + rx1[0] + rx2[...].astype(F32)).astype(BF16)
-
-    height = pk.shape[1]
-    lanes = lax.broadcasted_iota(I32, (height, summed.shape[0]), 1)
+    def rows_of(q):
+        return pl.ds(pl.multiple_of(q * chunk_rows, chunk_rows), chunk_rows)
+
+    def first(q):
+        r = rows_of(q)
+        return remote(part.at[cross, r], rx1.at[1, r], ns.at[0, q], nr.at[0, q], (wide, near))
+
+    def second(q):
+        r = rows_of(q)
+        return remote(part.at[near, r], rx1.at[0, r], ns.at[1, q], nr.at[1, q], (wide, near))
+
+    def third(q):
+        r = rows_of(q)
+        return remote(tx2.at[r], rx2.at[r], ns.at[2, q], nr.at[2, q], (wide, far))
+
+    def relay(q):
+        r = rows_of(q)
+        first(q).wait()
+        tx2[r] = (part[far, r] + rx1[1, r]).astype(BF16)
+        third(q).start()
+
+    def finish(q):
+        r = rows_of(q)
+        second(q).wait()
+        third(q).wait()
+        summed[r] = (part[me, r] + rx1[0, r] + rx2[r].astype(F32)).astype(BF16)
 
     def send(d):
         other = (wide + d) % count
@@ -225,55 +186,124 @@
         )
 
     def packed(d):
+        lanes = lax.broadcasted_iota(I32, (height, summed.shape[0]), 1)
         pick = (src_ref[(wide + d) % count] == lanes).astype(F32).astype(BF16)
         pk[d] = jnp.dot(pick, summed[...], preferred_element_type=F32).astype(BF16)
 
-    @pl.loop(1, count)
-    def _(d):
-        packed(d)
-        for copy in send(d):
-            copy.start()
-
-    packed(0)
-    places = lax.broadcasted_iota(I32, (out_ref.shape[0], height), 0)
-
     def placed(labels, rows):
+        places = lax.broadcasted_iota(I32, (out_ref.shape[0], height), 0)
         pick = (labels == places).astype(F32).astype(BF16)
         return jnp.dot(pick, rows, preferred_element_type=F32)
 
-    out_ref[...] = placed(lab_ref[wide], pk[0])
-
-    @pl.loop(1, count)
-    def _(d):
-        for copy in send(d):
-            copy.wait()
-        out_ref[...] += placed(rxl[d], rxw[d])
-
-
-def exchange(part, src, lab, parts, side):
-    rows, columns = part.shape[1:]
+    @pl.when(step == 0)
+    def _():
+        barrier = pltpu.get_barrier_semaphore()
+        pl.semaphore_signal(barrier, inc=1, device_id=(wide, near), device_id_type=MESH)
+        pl.semaphore_signal(barrier, inc=1, device_id=(wide, far), device_id_type=MESH)
+
+        @pl.loop(1, count)
+        def _(d):
+            pl.semaphore_signal(
+                barrier, inc=1, device_id=((wide + d) % count, me), device_id_type=MESH
+            )
+
+        pl.semaphore_wait(barrier, count + 1)
+
+    lane_half = lax.broadcasted_iota(I32, (1, 2 * HALF), 1) // HALF
+    rows = []
+    for j in range(QUAD):
+        base = (step * QUAD + j) * terms
+        applied = [
+            jnp.dot(op_ref[j, k], near_ref[tile_ref[base + k]], preferred_element_type=F32).astype(BF16)
+            for k in range(terms)
+        ]
+        projected = jnp.dot(own_ref[j], jnp.concatenate(applied, axis=1), preferred_element_type=F32)
+        sums = [jnp.zeros((M, 2 * HALF), F32) for _ in range(KC // 2)]
+        for k in range(terms):
+            slot = slot_ref[base + k]
+            piece = projected[:, k * 2 * HALF : (k + 1) * 2 * HALF]
+            piece = jnp.where(swap_ref[base + k] == 1, pltpu.roll(piece, HALF, 1), piece)
+            for t in range(KC // 2):
+                sums[t] = sums[t] + jnp.where(lane_half + 2 * t == slot, piece, 0.0)
+        rows.append(
+            jnp.concatenate(
+                [sums[s // 2][:, (s % 2) * HALF : (s % 2) * HALF + M] for s in range(KC)], axis=1
+            )
+        )
+    at = pl.ds(pl.multiple_of(step * (QUAD * side), QUAD * side), QUAD * side)
+    for g in range(parts):
+        part[g, at] = jnp.concatenate([row[g * side : (g + 1) * side] for row in rows], axis=0)
+
+    @pl.when(step % per == per - 1)
+    def _():
+        first(step // per).start()
+        second(step // per).start()
+
+    @pl.when((step % per == per // 2) & (step >= per))
+    def _():
+        relay(step // per - 1)
+
+    @pl.when(step == steps - 1)
+    def _():
+        relay(chunks - 1)
+        for q in range(chunks):
+            finish(q)
+
+        @pl.loop(1, count)
+        def _(d):
+            packed(d)
+            for copy in send(d):
+                copy.start()
+
+        packed(0)
+        out_ref[...] = placed(lab_ref[wide], pk[0])
+
+        @pl.loop(1, count)
+        def _(d):
+            for copy in send(d):
+                copy.wait()
+            out_ref[...] += placed(rxl[d], rxw[d])
+
+
+def coarse_rows(op_blocks, near, own, tiles, swaps, slots, src, lab, parts, chunks=4):
+    count_rows, terms, part_rows, _ = op_blocks.shape
+    side = M // parts
     count, _, height = lab.shape
+    steps = count_rows // QUAD
+    rows, columns = count_rows * side, KC * M
     vmem = pl.BlockSpec(memory_space=pltpu.VMEM)
     dma = pltpu.SemaphoreType.DMA
     return pl.pallas_call(
-        functools.partial(exchange_kernel, count, parts),
+        functools.partial(coarse_kernel, count, parts, terms, steps, chunks),
         out_shape=jax.ShapeDtypeStruct((AGG_DEV * side, columns), F32),
-        in_specs=[vmem] * 3,
-        out_specs=vmem,
-        scratch_shapes=[
-            pltpu.VMEM((2, rows, columns), F32),
-            pltpu.VMEM((rows, columns), BF16),
-            pltpu.VMEM((rows, columns), BF16),
-            pltpu.VMEM((count, height, columns), BF16),
-            pltpu.VMEM((count, height, columns), BF16),
-            pltpu.VMEM((count, 1, height), I32),
-            pltpu.VMEM((rows, columns), BF16),
-            dma((3,)), dma((3,)), dma((count,)), dma((count,)), dma((count,)), dma((count,)),
-        ],
+        grid_spec=pltpu.PrefetchScalarGridSpec(
+            num_scalar_prefetch=3,
+            grid=(steps,),
+            in_specs=[
+                pl.BlockSpec((QUAD, terms, part_rows, B), lambda i, *_: (i, 0, 0, 0)),
+                vmem,
+                pl.BlockSpec((QUAD, M, part_rows), lambda i, *_: (i, 0, 0)),
+                vmem,
+                vmem,
+            ],
+            out_specs=pl.BlockSpec((AGG_DEV * side, columns), lambda i, *_: (0, 0)),
+            scratch_shapes=[
+                pltpu.VMEM((parts, rows, columns), F32),
+                pltpu.VMEM((2, rows, columns), F32),
+                pltpu.VMEM((rows, columns), BF16),
+                pltpu.VMEM((rows, columns), BF16),
+                pltpu.VMEM((count, height, columns), BF16),
+                pltpu.VMEM((count, height, columns), BF16),
+                pltpu.VMEM((count, 1, height), I32),
+                pltpu.VMEM((rows, columns), BF16),
+                dma((3, chunks)), dma((3, chunks)),
+                dma((count,)), dma((count,)), dma((count,)), dma((count,)),
+            ],
+        ),
         compiler_params=pltpu.CompilerParams(
             collective_id=0, has_side_effects=True, vmem_limit_bytes=48 << 20
         ),
-    )(part, src, lab)
+    )(tiles, swaps, slots, op_blocks, near, own, src, lab)
 
 
 def routes(owner, local, count, capacity, side):
@@ -314,8 +344,9 @@
     inner = cols % count_rows
     tiles = cols // count_rows * pairs + inner % pairs
     swaps = (inner // pairs + slots) % 2
-    part = products(op_blocks, near, blocks.swapaxes(1, 2), tiles, swaps, slots, parts)
-    coarse = exchange(part, src, lab, parts, side)
+    coarse = coarse_rows(
+        op_blocks, near, blocks.swapaxes(1, 2), tiles, swaps, slots, src, lab, parts
+    )
     return coarse.reshape(AGG_DEV, side, KC * M)
 
 

time: 118 us -> 106 us (0.90)
  Pallas kernels: 106 us -> 95.9 us
  local copies, waits for them, and re-layouts: 9.72 us -> 6.87 us
    pallas_call x2 -> x1, Pallas kernels: 71.3 us -> 61.4 us  [coarse_rows(): pl.pallas_call(functools.partial(coarse_kernel, count, parts, terms, step...]
    unnamed x15 -> x5, local copies, waits for them, and re-layouts: 4.57 us -> 0.81 us
where the time goes in v3:
time: 106 us
  Pallas kernels  95.9 us (90%)
  local copies, waits for them, and re-layouts  6.87 us (6%)
  other arithmetic  2.61 us (2%)
    pallas_call x1, Pallas kernels, coarse_rows(): pl.pallas_call(functools.partial(coarse_kernel, count, parts, terms, step...  61.4 us
    pallas_call x1, Pallas kernels, gathered(): pl.pallas_call(functools.partial(gather_kernel, count, parts, chunks), ou...  34.5 us
    reshape x2, local copies, waits for them, and re-layouts, on_device(): blocks = prolong.reshape(count_rows, part_rows, M)  2.38 us

profile of v3, /device:TPU:13, one launch (start us, length us, event | category | flops | bytes accessed | tf_op | source)
XLA Modules:
  0.0 105.6 jit_solution(13350262150719324901)
XLA Ops:
  0.0 0.0 copy-start
  0.0 0.0 copy-start.1
  0.0 0.8 copy.22
  0.8 0.1 reshape.185.slot_ref
  1.0 0.7 subtract_add_fusion
  1.6 0.1 copy.21
  1.7 0.1 reshape.184
  1.9 1.0 fusion.12
  2.9 0.6 slice.15
  3.5 0.6 slice.13
  4.0 0.1 broadcast_in_dim.52
  4.1 1.2 %pad_maximum_fusion.own_ref = bf16[32,48,128]{2,1,0:T(8,128)(2,1)} fusion(bf16[32,48,16]{2,1,0:T(8,128)(2,1)S(1)} %broadcast_in_dim.52, bf16[32,48,48]{2,1,0:T(8,128)(2,1)S(1)} %slice.15, bf16[32,48,48]{2,1,0:T(8,128)(2,1)S(1)} %slice.13), kind=kLoop, calls=%fused_computation.5 | loop fusion | flops 1572864 | bytes 737280 | tf_op jit(solution)/shard_map/concatenate | solution.py:340
  5.3 34.5 %shard_map.64.near_ref = bf16[96,192,128]{2,1,0:T(8,128)(2,1)} custom-call(bf16[32,48,128]{2,1,0:T(8,128)(2,1)} %pad_maximum_fusion.own_ref), custom_call_target="tpu_custom_call" | custom-call | tf_op jit(solution)/shard_map/pallas_call | solution.py:123
  39.8 2.0 %reshape.186 = bf16[64,48,48]{2,1,0:T(8,128)(2,1)S(1)} reshape(bf16[64,2304]{1,0:T(8,128)(2,1)} %param.7) | data formatting | bytes 589824 | tf_op jit(solution)/shard_map/reshape | solution.py:338
  41.9 0.4 copy.23
  42.3 0.1 add_select_fusion
  42.3 0.0 copy-done.1
  42.3 0.2 convert_reduce_fusion
  42.5 0.0 copy-done
  42.5 0.2 fusion.1
  42.7 0.1 compare_reduce_fusion
  42.9 0.3 copy.25.src_ref
  43.3 61.4 %shard_map.65 = f32[192,384]{1,0:T(8,128)S(1)} custom-call(s32[384]{0:T(512)S(1)} %get-tuple-element.10.tile_ref, s32[384]{0:T(512)S(1)} %get-tuple-element.9.swap_ref, s32[384]{0:T(512)S(1)} %reshape.185.slot_ref, bf16[64,6,48,192]{3,2,1,0:T(8,128)(2,1)} %op_ref.1, bf16[96,192,128]{2,1,0:T(8,128)(2,1)} %shard_map.64.near_ref, ...), custom_call_target="tpu_custom_call" | custom-call | tf_op jit(solution)/shard_map/pallas_call | solution.py:276
  104.8 0.8 copy.26
  (10 shorter events, 0.1 us)
Async XLA Ops:
  0.0 42.5 %copy-start = (s32[64]{0:T(128)S(1)}, s32[64]{0:T(128)}, u32[]{:S(2)}) copy-start(s32[64]{0:T(128)} %param.11) | copy-start | bytes 772
  0.0 42.3 %copy-start.1 = (s32[64,1]{0,1:T(1,128)S(1)}, s32[64,1]{0,1:T(1,128)}, u32[]{:S(2)}) copy-start(s32[64,1]{0,1:T(1,128)} %param.10) | copy-start | bytes 772

commit v4 on v3

--- a/solution.py
+++ b/solution.py
@@ -13,6 +13,7 @@
 AGG_DEV = 16
 HALF = 64
 QUAD = 4
+ROWS = 8
 MESH = pl.DeviceIdType.MESH
 F32 = jnp.float32
 BF16 = jnp.bfloat16
@@ -46,11 +47,11 @@
     def place(slot, part, c):
         return near_ref.at[pl.ds(slot * pairs + c * piece, piece), pl.ds(part * depth, depth)]
 
-    def remote(slot, kind, c, target, source, part):
+    def remote(slot, kind, c, target, source, part, sent=None):
         return pltpu.make_async_remote_copy(
             src_ref=source,
             dst_ref=place(slot, part, c),
-            send_sem=ss.at[slot, kind, c],
+            send_sem=ss.at[slot, kind if sent is None else sent, c],
             recv_sem=rs.at[slot, kind, c],
             device_id=target,
             device_id_type=MESH,
@@ -85,14 +86,28 @@
         to_near(1, c).start()
     keep.start()
 
+    def across(slot, c):
+        target = (wide + 1 if slot == 0 else wide - 1, me)
+        return remote(slot, 2, c, target, place(1, far, c), far, sent=4)
+
+    twin = {0: has[2] & (wide % 2 == 0), 2: wide % 2 == 1}
+    paired = {0: wide % 2 == 1, 2: has[2] & (wide % 2 == 0)}
+    detour = [c for c in range(chunks) if c < chunks // 2]
+
     def spread(slot, c):
         direct(slot, c).wait_recv()
-        to_far(slot, c).start()
         to_near(slot, c).start()
+        if c in detour:
+            pl.when(jnp.logical_not(paired[slot]))(lambda: to_far(slot, c).start())
+        else:
+            to_far(slot, c).start()
 
     def forward(slot, c):
         to_far(slot, c).wait_recv()
         onward(slot, c).start()
+        if slot == 1 and c in detour:
+            for there in (0, 2):
+                pl.when(twin[there])(lambda: across(there, c).start())
 
     for c in range(chunks):
         forward(1, c)
@@ -105,11 +120,17 @@
     def drain(slot):
         for c in range(chunks):
             to_near(slot, c).wait()
-            to_far(slot, c).wait_send()
+            if slot != 1 and c in detour:
+                pl.when(jnp.logical_not(paired[slot]))(lambda: to_far(slot, c).wait_send())
+            else:
+                to_far(slot, c).wait_send()
             onward(slot, c).wait()
 
     for slot in range(3):
         when(has[slot], lambda: drain(slot))
+    for c in detour:
+        for there in (0, 2):
+            pl.when(twin[there])(lambda: across(there, c).wait_send())
     for c in range(chunks):
         when(has[2], lambda: direct(0, c).wait_send())
         when(has[0], lambda: direct(2, c).wait_send())
@@ -119,7 +140,7 @@
 def gathered(own, count, parts, chunks=4):
     pairs, depth, lanes = own.shape
     hbm = pl.BlockSpec(memory_space=pl.ANY)
-    sems = pltpu.SemaphoreType.DMA((3, 4, chunks))
+    sems = pltpu.SemaphoreType.DMA((3, 5, chunks))
     return pl.pallas_call(
         functools.partial(gather_kernel, count, parts, chunks),
         out_shape=jax.ShapeDtypeStruct((3 * pairs, parts * depth, lanes), BF16),
@@ -210,14 +231,23 @@
         pl.semaphore_wait(barrier, count + 1)
 
     lane_half = lax.broadcasted_iota(I32, (1, 2 * HALF), 1) // HALF
+    applied = []
+    for j in range(ROWS):
+        base = (step * ROWS + j) * terms
+        for k in range(0, terms, 2):
+            tiles = jnp.concatenate(
+                [near_ref[tile_ref[base + k]], near_ref[tile_ref[base + k + 1]]], axis=1
+            )
+            stacked = op_ref[j, k : k + 2].reshape(-1, B)
+            both = jnp.dot(stacked, tiles, preferred_element_type=F32)
+            depth = both.shape[0] // 2
+            applied.append(both[:depth, : 2 * HALF].astype(BF16))
+            applied.append(both[depth:, 2 * HALF :].astype(BF16))
     rows = []
-    for j in range(QUAD):
-        base = (step * QUAD + j) * terms
-        applied = [
-            jnp.dot(op_ref[j, k], near_ref[tile_ref[base + k]], preferred_element_type=F32).astype(BF16)
-            for k in range(terms)
-        ]
-        projected = jnp.dot(own_ref[j], jnp.concatenate(applied, axis=1), preferred_element_type=F32)
+    for j in range(ROWS):
+        base = (step * ROWS + j) * terms
+        held = jnp.concatenate(applied[j * terms : (j + 1) * terms], axis=1)
+        projected = jnp.dot(own_ref[j], held, preferred_element_type=F32)
         sums = [jnp.zeros((M, 2 * HALF), F32) for _ in range(KC // 2)]
         for k in range(terms):
             slot = slot_ref[base + k]
@@ -230,9 +260,13 @@
                 [sums[s // 2][:, (s % 2) * HALF : (s % 2) * HALF + M] for s in range(KC)], axis=1
             )
         )
-    at = pl.ds(pl.multiple_of(step * (QUAD * side), QUAD * side), QUAD * side)
-    for g in range(parts):
-        part[g, at] = jnp.concatenate([row[g * side : (g + 1) * side] for row in rows], axis=0)
+    block = QUAD * side
+    for b in range(ROWS // QUAD):
+        at = pl.ds(pl.multiple_of(step * (ROWS * side) + b * block, block), block)
+        for g in range(parts):
+            part[g, at] = jnp.concatenate(
+                [row[g * side : (g + 1) * side] for row in rows[b * QUAD : (b + 1) * QUAD]], axis=0
+            )
 
     @pl.when(step % per == per - 1)
     def _():
@@ -269,7 +303,7 @@
     count_rows, terms, part_rows, _ = op_blocks.shape
     side = M // parts
     count, _, height = lab.shape
-    steps = count_rows // QUAD
+    steps = count_rows // ROWS
     rows, columns = count_rows * side, KC * M
     vmem = pl.BlockSpec(memory_space=pltpu.VMEM)
     dma = pltpu.SemaphoreType.DMA
@@ -280,9 +314,9 @@
             num_scalar_prefetch=3,
             grid=(steps,),
             in_specs=[
-                pl.BlockSpec((QUAD, terms, part_rows, B), lambda i, *_: (i, 0, 0, 0)),
+                pl.BlockSpec((ROWS, terms, part_rows, B), lambda i, *_: (i, 0, 0, 0)),
                 vmem,
-                pl.BlockSpec((QUAD, M, part_rows), lambda i, *_: (i, 0, 0)),
+                pl.BlockSpec((ROWS, M, part_rows), lambda i, *_: (i, 0, 0)),
                 vmem,
                 vmem,
             ],

time: 106 us -> 95.4 us (0.900)
  Pallas kernels: 95.9 us -> 85.6 us
    pallas_call x1, Pallas kernels: 61.4 us -> 54 us  [coarse_rows(): pl.pallas_call(functools.partial(coarse_kernel, count, parts, terms, step...]
    pallas_call x1, Pallas kernels: 34.5 us -> 31.5 us  [gathered(): pl.pallas_call(functools.partial(gather_kernel, count, parts, chunks), ou...]
where the time goes in v4:
time: 95.4 us; the launch traced here: 95.2 us
  Pallas kernels  85.6 us (90%)
  local copies, waits for them, and re-layouts  6.87 us (7%)
  other arithmetic  2.61 us (3%)
    pallas_call x1, Pallas kernels, coarse_rows(): pl.pallas_call(functools.partial(coarse_kernel, count, parts, terms, step...  54 us
    pallas_call x1, Pallas kernels, gathered(): pl.pallas_call(functools.partial(gather_kernel, count, parts, chunks), ou...  31.5 us
    reshape x2, local copies, waits for them, and re-layouts, on_device(): blocks = prolong.reshape(count_rows, part_rows, M)  2.38 us
    slice x3, local copies, waits for them, and re-layouts, on_device(): paired = jnp.concatenate([blocks[:pairs], gap, blocks[pairs:], gap], axis=2)  2.11 us

profile of v4, /device:TPU:13, one launch (start us, length us, event | category | flops | bytes accessed | tf_op | source)
XLA Modules:
  0.0 95.2 jit_solution(17813464713293726965)
XLA Ops:
  0.0 0.0 copy-start
  0.0 0.0 copy-start.1
  0.0 0.8 copy.22
  0.8 0.1 reshape.185.slot_ref
  1.0 0.7 subtract_add_fusion
  1.6 0.1 copy.21
  1.7 0.1 reshape.184
  1.9 1.0 %fusion.12 = (bf16[32,2304]{1,0:T(8,128)(2,1)S(1)}, bf16[32,2304]{1,0:T(8,128)(2,1)S(1)}) fusion(bf16[64,2304]{1,0:T(8,128)(2,1)} %param.7), kind=kLoop, calls=%fused_computation.48 | loop fusion | bytes 589824 | tf_op jit(solution)/shard_map/slice | solution.py:374
  2.9 0.6 slice.15
  3.5 0.6 slice.13
  4.0 0.1 broadcast_in_dim.52
  4.1 1.2 %pad_maximum_fusion.own_ref = bf16[32,48,128]{2,1,0:T(8,128)(2,1)} fusion(bf16[32,48,16]{2,1,0:T(8,128)(2,1)S(1)} %broadcast_in_dim.52, bf16[32,48,48]{2,1,0:T(8,128)(2,1)S(1)} %slice.15, bf16[32,48,48]{2,1,0:T(8,128)(2,1)S(1)} %slice.13), kind=kLoop, calls=%fused_computation.5 | loop fusion | flops 1572864 | bytes 737280 | tf_op jit(solution)/shard_map/concatenate | solution.py:374
  5.3 31.5 %shard_map.64.near_ref = bf16[96,192,128]{2,1,0:T(8,128)(2,1)} custom-call(bf16[32,48,128]{2,1,0:T(8,128)(2,1)} %pad_maximum_fusion.own_ref), custom_call_target="tpu_custom_call" | custom-call | tf_op jit(solution)/shard_map/pallas_call | solution.py:144
  36.9 2.0 %reshape.186 = bf16[64,48,48]{2,1,0:T(8,128)(2,1)S(1)} reshape(bf16[64,2304]{1,0:T(8,128)(2,1)} %param.7) | data formatting | bytes 589824 | tf_op jit(solution)/shard_map/reshape | solution.py:372
  38.9 0.4 copy.23
  39.3 0.1 add_select_fusion
  39.4 0.0 copy-done.1
  39.4 0.2 convert_reduce_fusion
  39.6 0.0 copy-done
  39.6 0.2 fusion.1
  39.8 0.1 compare_reduce_fusion
  40.0 0.3 copy.25.src_ref
  40.3 54.0 %shard_map.65 = f32[192,384]{1,0:T(8,128)S(1)} custom-call(s32[384]{0:T(512)S(1)} %get-tuple-element.10.tile_ref, s32[384]{0:T(512)S(1)} %get-tuple-element.9.swap_ref, s32[384]{0:T(512)S(1)} %reshape.185.slot_ref, bf16[64,6,48,192]{3,2,1,0:T(8,128)(2,1)} %op_ref.1, bf16[96,192,128]{2,1,0:T(8,128)(2,1)} %shard_map.64.near_ref, ...), custom_call_target="tpu_custom_call" | custom-call | tf_op jit(solution)/shard_map/pallas_call | solution.py:310
  94.4 0.8 copy.26
  (10 shorter events, 0.1 us)
Async XLA Ops:
  0.0 39.6 %copy-start = (s32[64]{0:T(128)S(1)}, s32[64]{0:T(128)}, u32[]{:S(2)}) copy-start(s32[64]{0:T(128)} %param.11) | copy-start | bytes 772
  0.0 39.4 %copy-start.1 = (s32[64,1]{0,1:T(1,128)S(1)}, s32[64,1]{0,1:T(1,128)}, u32[]{:S(2)}) copy-start(s32[64,1]{0,1:T(1,128)} %param.10) | copy-start | bytes 772

commit v5 on v4

--- a/solution.py
+++ b/solution.py
@@ -277,14 +277,24 @@
     def _():
         relay(step // per - 1)
 
+    lag = 3
+
+    @pl.when((step % per == per - 1) & (step >= lag * per))
+    def _():
+        finish(step // per - lag)
+
     @pl.when(step == steps - 1)
     def _():
         relay(chunks - 1)
-        for q in range(chunks):
+        for q in range(chunks - lag, chunks):
             finish(q)
 
-        @pl.loop(1, count)
-        def _(d):
+        def turn(i):
+            return 1 + (i + count // 2 - 1) % (count - 1)
+
+        @pl.loop(0, count - 1)
+        def _(i):
+            d = turn(i)
             packed(d)
             for copy in send(d):
                 copy.start()
@@ -292,14 +302,15 @@
         packed(0)
         out_ref[...] = placed(lab_ref[wide], pk[0])
 
-        @pl.loop(1, count)
-        def _(d):
+        @pl.loop(0, count - 1)
+        def _(i):
+            d = turn(i)
             for copy in send(d):
                 copy.wait()
             out_ref[...] += placed(rxl[d], rxw[d])
 
 
-def coarse_rows(op_blocks, near, own, tiles, swaps, slots, src, lab, parts, chunks=4):
+def coarse_rows(op_blocks, near, own, tiles, swaps, slots, src, lab, parts, chunks=8):
     count_rows, terms, part_rows, _ = op_blocks.shape
     side = M // parts
     count, _, height = lab.shape

time: 95.4 us -> 95.7 us (level)
  the two profiles are of different devices: /device:TPU:13 before, /device:TPU:0 now
where the time goes in v5:
time: 95.7 us; the launch traced here: 95.4 us
  Pallas kernels  85.8 us (90%)
  local copies, waits for them, and re-layouts  6.87 us (7%)
  other arithmetic  2.61 us (3%)
    pallas_call x1, Pallas kernels, coarse_rows(): pl.pallas_call(functools.partial(coarse_kernel, count, parts, terms, step...  60.4 us
    pallas_call x1, Pallas kernels, gathered(): pl.pallas_call(functools.partial(gather_kernel, count, parts, chunks), ou...  25.4 us
    reshape x2, local copies, waits for them, and re-layouts, on_device(): blocks = prolong.reshape(count_rows, part_rows, M)  2.38 us
    slice x3, local copies, waits for them, and re-layouts, on_device(): paired = jnp.concatenate([blocks[:pairs], gap, blocks[pairs:], gap], axis=2)  2.11 us

profile of v5, /device:TPU:0, one launch (start us, length us, event | category | flops | bytes accessed | tf_op | source)
XLA Modules:
  0.0 95.4 jit_solution(11845888189934557742)
XLA Ops:
  0.0 0.0 copy-start
  0.0 0.0 copy-start.1
  0.0 0.8 copy.22
  0.8 0.1 reshape.185.slot_ref
  1.0 0.7 subtract_add_fusion
  1.6 0.1 copy.21
  1.7 0.1 reshape.184
  1.9 1.0 %fusion.12 = (bf16[32,2304]{1,0:T(8,128)(2,1)S(1)}, bf16[32,2304]{1,0:T(8,128)(2,1)S(1)}) fusion(bf16[64,2304]{1,0:T(8,128)(2,1)} %param.7), kind=kLoop, calls=%fused_computation.48 | loop fusion | bytes 589824 | tf_op jit(solution)/shard_map/slice | solution.py:385
  2.9 0.6 slice.15
  3.5 0.6 slice.13
  4.0 0.1 broadcast_in_dim.52
  4.1 1.2 %pad_maximum_fusion.own_ref = bf16[32,48,128]{2,1,0:T(8,128)(2,1)} fusion(bf16[32,48,16]{2,1,0:T(8,128)(2,1)S(1)} %broadcast_in_dim.52, bf16[32,48,48]{2,1,0:T(8,128)(2,1)S(1)} %slice.15, bf16[32,48,48]{2,1,0:T(8,128)(2,1)S(1)} %slice.13), kind=kLoop, calls=%fused_computation.5 | loop fusion | flops 1572864 | bytes 737280 | tf_op jit(solution)/shard_map/concatenate | solution.py:385
  5.3 25.4 %shard_map.64.near_ref = bf16[96,192,128]{2,1,0:T(8,128)(2,1)} custom-call(bf16[32,48,128]{2,1,0:T(8,128)(2,1)} %pad_maximum_fusion.own_ref), custom_call_target="tpu_custom_call" | custom-call | tf_op jit(solution)/shard_map/pallas_call | solution.py:144
  30.8 2.0 %reshape.186 = bf16[64,48,48]{2,1,0:T(8,128)(2,1)S(1)} reshape(bf16[64,2304]{1,0:T(8,128)(2,1)} %param.7) | data formatting | bytes 589824 | tf_op jit(solution)/shard_map/reshape | solution.py:383
  32.8 0.4 copy.23
  33.2 0.1 add_select_fusion
  33.3 0.0 copy-done.1
  33.3 0.2 convert_reduce_fusion
  33.5 0.0 copy-done
  33.5 0.2 fusion.1
  33.7 0.1 compare_reduce_fusion
  33.9 0.3 copy.25.src_ref
  34.2 60.4 %shard_map.65 = f32[192,384]{1,0:T(8,128)S(1)} custom-call(s32[384]{0:T(512)S(1)} %get-tuple-element.10.tile_ref, s32[384]{0:T(512)S(1)} %get-tuple-element.9.swap_ref, s32[384]{0:T(512)S(1)} %reshape.185.slot_ref, bf16[64,6,48,192]{3,2,1,0:T(8,128)(2,1)} %op_ref.1, bf16[96,192,128]{2,1,0:T(8,128)(2,1)} %shard_map.64.near_ref, ...), custom_call_target="tpu_custom_call" | custom-call | tf_op jit(solution)/shard_map/pallas_call | solution.py:321
  94.6 0.8 copy.26
  (10 shorter events, 0.1 us)
Async XLA Ops:
  0.0 33.5 %copy-start = (s32[64]{0:T(128)S(1)}, s32[64]{0:T(128)}, u32[]{:S(2)}) copy-start(s32[64]{0:T(128)} %param.11) | copy-start | bytes 772
  0.0 33.3 %copy-start.1 = (s32[64,1]{0,1:T(1,128)S(1)}, s32[64,1]{0,1:T(1,128)}, u32[]{:S(2)}) copy-start(s32[64,1]{0,1:T(1,128)} %param.10) | copy-start | bytes 772

commit v6 on v5

--- a/solution.py
+++ b/solution.py
@@ -153,8 +153,8 @@
 
 def coarse_kernel(
     count, parts, terms, steps, chunks,
-    tile_ref, swap_ref, slot_ref, op_ref, near_ref, own_ref, src_ref, lab_ref, out_ref,
-    part, rx1, tx2, rx2, pk, rxw, rxl, summed, ns, nr, ws, wr, ls, lr,
+    tile_ref, swap_ref, slot_ref, op_ref, near_ref, own_ref, key_ref, out_ref,
+    part, rx1, tx2, rx2, pk, rxw, rxk, summed, rxs, ns, nr, ys, yr, ws, wr, ks,
 ):
     step = pl.program_id(0)
     wide = lax.axis_index("wide")
@@ -164,6 +164,8 @@
     cross = (near + 2) % parts
     side = M // parts
     per = steps // chunks
+    half = count // 2
+    twin = wide + 1 - 2 * (wide % 2)
     height = pk.shape[1]
     chunk_rows = summed.shape[0] // chunks
 
@@ -199,22 +201,23 @@
         third(q).wait()
         summed[r] = (part[me, r] + rx1[0, r] + rx2[r].astype(F32)).astype(BF16)
 
+    def fourth(q):
+        r = rows_of(q)
+        return remote(summed.at[r], rxs.at[r], ys.at[q], yr.at[q], (twin, me))
+
+    def keys():
+        return remote(key_ref, rxk, ks.at[0], ks.at[1], (twin, me))
+
     def send(d):
-        other = (wide + d) % count
-        return (
-            remote(pk.at[d], rxw.at[d], ws.at[d], wr.at[d], (other, me)),
-            remote(lab_ref.at[other], rxl.at[d], ls.at[d], lr.at[d], (other, me)),
+        return remote(pk.at[d], rxw.at[d], ws.at[d], wr.at[d], ((wide + 2 * d) % count, me))
+
+    def dense(owner):
+        places = lax.broadcasted_iota(I32, (height, summed.shape[0]), 0) + owner * height
+        ours = (key_ref[...] == places).astype(F32).astype(BF16)
+        theirs = (rxk[...] == places).astype(F32).astype(BF16)
+        return jnp.dot(ours, summed[...], preferred_element_type=F32) + jnp.dot(
+            theirs, rxs[...], preferred_element_type=F32
         )
-
-    def packed(d):
-        lanes = lax.broadcasted_iota(I32, (height, summed.shape[0]), 1)
-        pick = (src_ref[(wide + d) % count] == lanes).astype(F32).astype(BF16)
-        pk[d] = jnp.dot(pick, summed[...], preferred_element_type=F32).astype(BF16)
-
-    def placed(labels, rows):
-        places = lax.broadcasted_iota(I32, (out_ref.shape[0], height), 0)
-        pick = (labels == places).astype(F32).astype(BF16)
-        return jnp.dot(pick, rows, preferred_element_type=F32)
 
     @pl.when(step == 0)
     def _():
@@ -222,13 +225,16 @@
         pl.semaphore_signal(barrier, inc=1, device_id=(wide, near), device_id_type=MESH)
         pl.semaphore_signal(barrier, inc=1, device_id=(wide, far), device_id_type=MESH)
 
-        @pl.loop(1, count)
+        pl.semaphore_signal(barrier, inc=1, device_id=(twin, me), device_id_type=MESH)
+
+        @pl.loop(1, half)
         def _(d):
             pl.semaphore_signal(
-                barrier, inc=1, device_id=((wide + d) % count, me), device_id_type=MESH
+                barrier, inc=1, device_id=((wide + 2 * d) % count, me), device_id_type=MESH
             )
 
-        pl.semaphore_wait(barrier, count + 1)
+        pl.semaphore_wait(barrier, half + 2)
+        keys().start()
 
     lane_half = lax.broadcasted_iota(I32, (1, 2 * HALF), 1) // HALF
     applied = []
@@ -277,43 +283,45 @@
     def _():
         relay(step // per - 1)
 
-    lag = 3
+    lag = 2
 
     @pl.when((step % per == per - 1) & (step >= lag * per))
     def _():
         finish(step // per - lag)
+        fourth(step // per - lag).start()
 
     @pl.when(step == steps - 1)
     def _():
         relay(chunks - 1)
         for q in range(chunks - lag, chunks):
             finish(q)
+            fourth(q).start()
+        keys().wait()
+        for q in range(chunks):
+            fourth(q).wait()
 
         def turn(i):
-            return 1 + (i + count // 2 - 1) % (count - 1)
-
-        @pl.loop(0, count - 1)
+            return 1 + (i + half // 2 - 1) % (half - 1)
+
+        @pl.loop(0, half - 1)
         def _(i):
             d = turn(i)
-            packed(d)
-            for copy in send(d):
-                copy.start()
-
-        packed(0)
-        out_ref[...] = placed(lab_ref[wide], pk[0])
-
-        @pl.loop(0, count - 1)
+            pk[d] = dense((wide + 2 * d) % count).astype(BF16)
+            send(d).start()
+
+        out_ref[...] = dense(wide)
+
+        @pl.loop(0, half - 1)
         def _(i):
             d = turn(i)
-            for copy in send(d):
-                copy.wait()
-            out_ref[...] += placed(rxl[d], rxw[d])
-
-
-def coarse_rows(op_blocks, near, own, tiles, swaps, slots, src, lab, parts, chunks=8):
+            send(d).wait()
+            out_ref[...] += rxw[d].astype(F32)
+
+
+def coarse_rows(op_blocks, near, own, tiles, swaps, slots, keys, count, parts, chunks=8):
     count_rows, terms, part_rows, _ = op_blocks.shape
     side = M // parts
-    count, _, height = lab.shape
+    height = AGG_DEV * side
     steps = count_rows // ROWS
     rows, columns = count_rows * side, KC * M
     vmem = pl.BlockSpec(memory_space=pltpu.VMEM)
@@ -329,7 +337,6 @@
                 vmem,
                 pl.BlockSpec((ROWS, M, part_rows), lambda i, *_: (i, 0, 0)),
                 vmem,
-                vmem,
             ],
             out_specs=pl.BlockSpec((AGG_DEV * side, columns), lambda i, *_: (0, 0)),
             scratch_shapes=[
@@ -337,38 +344,19 @@
                 pltpu.VMEM((2, rows, columns), F32),
                 pltpu.VMEM((rows, columns), BF16),
                 pltpu.VMEM((rows, columns), BF16),
-                pltpu.VMEM((count, height, columns), BF16),
-                pltpu.VMEM((count, height, columns), BF16),
-                pltpu.VMEM((count, 1, height), I32),
+                pltpu.VMEM((count // 2, height, columns), BF16),
+                pltpu.VMEM((count // 2, height, columns), BF16),
+                pltpu.VMEM((1, rows), I32),
                 pltpu.VMEM((rows, columns), BF16),
-                dma((3, chunks)), dma((3, chunks)),
-                dma((count,)), dma((count,)), dma((count,)), dma((count,)),
+                pltpu.VMEM((rows, columns), BF16),
+                dma((3, chunks)), dma((3, chunks)), dma((chunks,)), dma((chunks,)),
+                dma((count // 2,)), dma((count // 2,)), dma((2,)),
             ],
         ),
         compiler_params=pltpu.CompilerParams(
             collective_id=0, has_side_effects=True, vmem_limit_bytes=48 << 20
         ),
-    )(tiles, swaps, slots, op_blocks, near, own, src, lab)
-
-
-def routes(owner, local, count, capacity, side):
-    rows = owner.shape[0]
-    index = jnp.arange(rows, dtype=I32)
-    earlier = (owner[:, None] == owner[None, :]) & (index[None, :] < index[:, None])
-    rank = jnp.sum(earlier.astype(I32), axis=1)
-    height = -(-capacity * side // 16) * 16
-    place = jnp.arange(height, dtype=I32)
-    wanted = jnp.arange(count, dtype=I32)[:, None] * capacity + place[None, :] // side
-    wanted = jnp.where(place[None, :] < capacity * side, wanted, -1)
-    match = wanted[:, :, None] == (owner * capacity + rank)[None, None, :]
-    filled = jnp.any(match, axis=2)
-    inner = place[None, :] % side
-
-    def spread(values):
-        picked = jnp.sum(jnp.where(match, values[None, None, :], 0), axis=2)
-        return jnp.where(filled, picked * side + inner, -1)
-
-    return spread(index)[:, :, None], spread(local)[:, None, :]
+    )(tiles, swaps, slots, op_blocks, near, own, keys)
 
 
 def on_device(op_blocks, prolong, col_index, slot_index, dest_owner, dest_local):
@@ -376,9 +364,9 @@
     count = lax.axis_size("wide")
     parts = lax.axis_size("narrow")
     wide_pos = lax.axis_index("wide")
-    capacity = max(2, 2 * count_rows // count)
     side = M // parts
-    src, lab = routes(dest_owner[:, 0], dest_local, count, capacity, side)
+    goal = (dest_owner[:, 0] * AGG_DEV + dest_local) * side
+    keys = (goal[:, None] + jnp.arange(side, dtype=I32)[None, :]).reshape(1, -1)
     pairs = count_rows // 2
     blocks = prolong.reshape(count_rows, part_rows, M)
     gap = jnp.zeros((pairs, part_rows, HALF - M), BF16)
@@ -390,7 +378,7 @@
     tiles = cols // count_rows * pairs + inner % pairs
     swaps = (inner // pairs + slots) % 2
     coarse = coarse_rows(
-        op_blocks, near, blocks.swapaxes(1, 2), tiles, swaps, slots, src, lab, parts
+        op_blocks, near, blocks.swapaxes(1, 2), tiles, swaps, slots, keys, count, parts
     )
     return coarse.reshape(AGG_DEV, side, KC * M)
 

time: 95.7 us -> 88.4 us (0.924)
  Pallas kernels: 85.8 us -> 76.3 us
  local copies, waits for them, and re-layouts: 6.87 us -> 8.97 us
    pallas_call x1, Pallas kernels: 60.4 us -> 50.9 us  [coarse_rows(): pl.pallas_call(functools.partial(coarse_kernel, count, parts, terms, step...]
    unnamed x5 -> x3, local copies, waits for them, and re-layouts: 0.81 us -> 3.11 us
where the time goes in v6:
time: 88.4 us; the launch traced here: 88.1 us
  Pallas kernels  76.3 us (86%)
  local copies, waits for them, and re-layouts  8.97 us (10%)
  other arithmetic  2.69 us (3%)
    pallas_call x1, Pallas kernels, coarse_rows(): pl.pallas_call(functools.partial(coarse_kernel, count, parts, terms, step...  50.9 us
    pallas_call x1, Pallas kernels, gathered(): pl.pallas_call(functools.partial(gather_kernel, count, parts, chunks), ou...  25.4 us
    unnamed x3, local copies, waits for them, and re-layouts  3.11 us
    reshape x2, local copies, waits for them, and re-layouts, on_device(): blocks = prolong.reshape(count_rows, part_rows, M)  2.38 us
    slice x3, local copies, waits for them, and re-layouts, on_device(): paired = jnp.concatenate([blocks[:pairs], gap, blocks[pairs:], gap], axis=2)  2.11 us

profile of v6, /device:TPU:0, one launch (start us, length us, event | category | flops | bytes accessed | tf_op | source)
XLA Modules:
  0.0 88.1 jit_solution(10753232382991737234)
XLA Ops:
  0.0 0.7 fusion.6
  0.7 0.7 subtract_add_fusion
  1.4 0.1 copy.8
  1.5 0.1 reshape.40
  1.6 0.1 iota_add_fusion
  1.7 0.1 add.65.key_ref
  1.8 0.8 copy.9
  2.6 0.1 reshape.41.slot_ref
  2.7 1.0 %fusion.7 = (bf16[32,2304]{1,0:T(8,128)(2,1)S(1)}, bf16[32,2304]{1,0:T(8,128)(2,1)S(1)}) fusion(bf16[64,2304]{1,0:T(8,128)(2,1)} %param.7), kind=kLoop, calls=%fused_computation.28 | loop fusion | bytes 589824 | tf_op jit(solution)/shard_map/slice | solution.py:373
  3.8 0.6 slice.13
  4.3 0.6 slice.15
  4.9 0.1 broadcast_in_dim.2
  4.9 1.2 %pad_maximum_fusion.own_ref = bf16[32,48,128]{2,1,0:T(8,128)(2,1)} fusion(bf16[32,48,16]{2,1,0:T(8,128)(2,1)S(1)} %broadcast_in_dim.2, bf16[32,48,48]{2,1,0:T(8,128)(2,1)S(1)} %slice.15, bf16[32,48,48]{2,1,0:T(8,128)(2,1)S(1)} %slice.13), kind=kLoop, calls=%fused_computation | loop fusion | flops 1572864 | bytes 737280 | tf_op jit(solution)/shard_map/concatenate | solution.py:373
  6.2 2.0 %reshape.42 = bf16[64,48,48]{2,1,0:T(8,128)(2,1)S(1)} reshape(bf16[64,2304]{1,0:T(8,128)(2,1)} %param.7) | data formatting | bytes 589824 | tf_op jit(solution)/shard_map/reshape | solution.py:371
  8.2 0.4 copy.10
  8.5 25.4 %shard_map.64.near_ref = bf16[96,192,128]{2,1,0:T(8,128)(2,1)} custom-call(bf16[32,48,128]{2,1,0:T(8,128)(2,1)} %pad_maximum_fusion.own_ref), custom_call_target="tpu_custom_call" | custom-call | tf_op jit(solution)/shard_map/pallas_call | solution.py:144
  34.0 0.0 copy-start
  34.0 2.3 %copy-done = bf16[96,192,128]{2,1,0:T(8,128)(2,1)S(1)} copy-done((bf16[96,192,128]{2,1,0:T(8,128)(2,1)S(1)}, bf16[96,192,128]{2,1,0:T(8,128)(2,1)}, u32[]{:S(2)}) %copy-start) | copy-done | bytes 4718616
  36.3 50.9 %shard_map.65 = f32[192,384]{1,0:T(8,128)S(1)} custom-call(s32[384]{0:T(512)S(1)} %get-tuple-element.8.tile_ref, s32[384]{0:T(512)S(1)} %get-tuple-element.7.swap_ref, s32[384]{0:T(512)S(1)} %reshape.41.slot_ref, bf16[64,6,48,192]{3,2,1,0:T(8,128)(2,1)} %op_ref.1, bf16[96,192,128]{2,1,0:T(8,128)(2,1)S(1)} %copy-done, bf16[64,48,48]{2,1,0:T(8,128)(2,1)S(1)} %bitcast.5, ...), custom_call_target="tpu_custom_call" | custom-call | tf_op jit(solution)/shard_map/pallas_call | solution.py:329
  87.3 0.8 copy.11
  (2 shorter events, 0.1 us)
Async XLA Ops:
  34.0 2.3 %copy-start = (bf16[96,192,128]{2,1,0:T(8,128)(2,1)S(1)}, bf16[96,192,128]{2,1,0:T(8,128)(2,1)}, u32[]{:S(2)}) copy-start(bf16[96,192,128]{2,1,0:T(8,128)(2,1)} %shard_map.64.near_ref) | copy-start | bytes 14155780

commit v7 on v6

--- a/solution.py
+++ b/solution.py
@@ -137,7 +137,7 @@
     keep.wait()
 
 
-def gathered(own, count, parts, chunks=4):
+def gathered(own, count, parts, chunks=8):
     pairs, depth, lanes = own.shape
     hbm = pl.BlockSpec(memory_space=pl.ANY)
     sems = pltpu.SemaphoreType.DMA((3, 5, chunks))

time: 88.4 us -> 88.6 us (level)
  the two profiles are of different devices: /device:TPU:0 before, /device:TPU:13 now
where the time goes in v7:
time: 88.6 us; the launch traced here: 88 us
  Pallas kernels  76.2 us (86%)
  local copies, waits for them, and re-layouts  8.97 us (10%)
  other arithmetic  2.69 us (3%)
    pallas_call x1, Pallas kernels, coarse_rows(): pl.pallas_call(functools.partial(coarse_kernel, count, parts, terms, step...  44.5 us
    pallas_call x1, Pallas kernels, gathered(): pl.pallas_call(functools.partial(gather_kernel, count, parts, chunks), ou...  31.8 us
    unnamed x3, local copies, waits for them, and re-layouts  3.11 us
    reshape x2, local copies, waits for them, and re-layouts, on_device(): blocks = prolong.reshape(count_rows, part_rows, M)  2.38 us
    slice x3, local copies, waits for them, and re-layouts, on_device(): paired = jnp.concatenate([blocks[:pairs], gap, blocks[pairs:], gap], axis=2)  2.11 us

profile of v7, /device:TPU:13, one launch (start us, length us, event | category | flops | bytes accessed | tf_op | source)
XLA Modules:
  0.0 88.0 jit_solution(15700669869614609638)
XLA Ops:
  0.0 0.7 fusion.6
  0.7 0.7 subtract_add_fusion
  1.4 0.1 copy.8
  1.5 0.1 reshape.40
  1.6 0.1 iota_add_fusion
  1.7 0.1 add.65.key_ref
  1.8 0.8 copy.9
  2.6 0.1 reshape.41.slot_ref
  2.7 1.0 %fusion.7 = (bf16[32,2304]{1,0:T(8,128)(2,1)S(1)}, bf16[32,2304]{1,0:T(8,128)(2,1)S(1)}) fusion(bf16[64,2304]{1,0:T(8,128)(2,1)} %param.7), kind=kLoop, calls=%fused_computation.28 | loop fusion | bytes 589824 | tf_op jit(solution)/shard_map/slice | solution.py:373
  3.8 0.6 slice.13
  4.3 0.6 slice.15
  4.9 0.1 broadcast_in_dim.2
  4.9 1.2 %pad_maximum_fusion.own_ref = bf16[32,48,128]{2,1,0:T(8,128)(2,1)} fusion(bf16[32,48,16]{2,1,0:T(8,128)(2,1)S(1)} %broadcast_in_dim.2, bf16[32,48,48]{2,1,0:T(8,128)(2,1)S(1)} %slice.15, bf16[32,48,48]{2,1,0:T(8,128)(2,1)S(1)} %slice.13), kind=kLoop, calls=%fused_computation | loop fusion | flops 1572864 | bytes 737280 | tf_op jit(solution)/shard_map/concatenate | solution.py:373
  6.2 2.0 %reshape.42 = bf16[64,48,48]{2,1,0:T(8,128)(2,1)S(1)} reshape(bf16[64,2304]{1,0:T(8,128)(2,1)} %param.7) | data formatting | bytes 589824 | tf_op jit(solution)/shard_map/reshape | solution.py:371
  8.2 0.4 copy.10
  8.5 31.8 %shard_map.64.near_ref = bf16[96,192,128]{2,1,0:T(8,128)(2,1)} custom-call(bf16[32,48,128]{2,1,0:T(8,128)(2,1)} %pad_maximum_fusion.own_ref), custom_call_target="tpu_custom_call" | custom-call | tf_op jit(solution)/shard_map/pallas_call | solution.py:144
  40.3 0.0 copy-start
  40.3 2.3 %copy-done = bf16[96,192,128]{2,1,0:T(8,128)(2,1)S(1)} copy-done((bf16[96,192,128]{2,1,0:T(8,128)(2,1)S(1)}, bf16[96,192,128]{2,1,0:T(8,128)(2,1)}, u32[]{:S(2)}) %copy-start) | copy-done | bytes 4718616
  42.6 44.5 %shard_map.65 = f32[192,384]{1,0:T(8,128)S(1)} custom-call(s32[384]{0:T(512)S(1)} %get-tuple-element.8.tile_ref, s32[384]{0:T(512)S(1)} %get-tuple-element.7.swap_ref, s32[384]{0:T(512)S(1)} %reshape.41.slot_ref, bf16[64,6,48,192]{3,2,1,0:T(8,128)(2,1)} %op_ref.1, bf16[96,192,128]{2,1,0:T(8,128)(2,1)S(1)} %copy-done, bf16[64,48,48]{2,1,0:T(8,128)(2,1)S(1)} %bitcast.5, ...), custom_call_target="tpu_custom_call" | custom-call | tf_op jit(solution)/shard_map/pallas_call | solution.py:329
  87.2 0.8 copy.11
  (2 shorter events, 0.1 us)
Async XLA Ops:
  40.3 2.3 %copy-start = (bf16[96,192,128]{2,1,0:T(8,128)(2,1)S(1)}, bf16[96,192,128]{2,1,0:T(8,128)(2,1)}, u32[]{:S(2)}) copy-start(bf16[96,192,128]{2,1,0:T(8,128)(2,1)} %shard_map.64.near_ref) | copy-start | bytes 14155780
